TPU v7x, 128 devices: a whole 4x4x4 slice. The times are simulated.
128 devices in a mesh: gx: 8 (over z_lo, x), gy: 8 (over y, core), gz: 2 (over z_hi).
Axes of the slice: x: 4, y: 4, z: 4 (z_hi: 2, z_lo: 2; z = z_hi * 2 + z_lo), core: 2. Of those that a mesh axis runs over, the one named last changes fastest.
Arguments:
- sol_pos: float32 [3, 8, 8, 2, 49152], P(None, 'gx', 'gy', 'gz'), as said below
- sol_vel: float32 [3, 8, 8, 2, 49152], P(None, 'gx', 'gy', 'gz'), may hold values from -6 to 6
- sol_rows: int32 [8, 8, 2], P('gx', 'gy', 'gz'), may hold values from 192 to 384, as said below
- mig_pos: float32 [3, 8, 8, 2, 6, 3072], P(None, 'gx', 'gy', 'gz'), as said below
- mig_vel: float32 [3, 8, 8, 2, 6, 3072], P(None, 'gx', 'gy', 'gz'), may hold values from -6 to 6
- mig_rows: int32 [8, 8, 2, 6], P('gx', 'gy', 'gz'), may hold values from 0 to 24, as said below
- bead_pos: float32 [3, 8, 8, 2, 256], P(None, 'gx', 'gy', 'gz'), as said below
- bead_vel: float32 [3, 8, 8, 2, 256], P(None, 'gx', 'gy', 'gz'), may hold values from -2.7 to 2.7
- bead_chains: int32 [8, 8, 2], P('gx', 'gy', 'gz'), may hold values from 5 to 32, as said below
- bond_list: int32 [2, 8, 8, 2, 224], P(None, 'gx', 'gy', 'gz'), may hold values from 0 to 255, as said below
- cell_axis: int32 [128, 128, 64], P('gx', 'gy', 'gz'), may hold values from 0 to 31
- shift: int32 [3], replicated, may hold values from 0 to 15
Outputs:
- sol_pos_out: float32 [3, 8, 8, 2, 67584], P(None, 'gx', 'gy', 'gz')
- sol_vel_out: float32 [3, 8, 8, 2, 67584], P(None, 'gx', 'gy', 'gz')
- bead_pos_out: float32 [3, 8, 8, 2, 256], P(None, 'gx', 'gy', 'gz')
- bead_vel_out: float32 [3, 8, 8, 2, 256], P(None, 'gx', 'gy', 'gz')
Inputs may be any that keep to these rules, and one draw needn't show every extreme that they name: `sol_rows`: some device's resident slots are all live. `mig_rows`: some device receives full buffers across all six faces. `sol_pos`: every resident position lies in its device's region (cells i * 16 to (i + 1) * 16 - 1 along the first dimension, likewise for the others), and x * 16 is at least 0.1 from a whole number. `mig_pos`: buffer f holds positions in the region of the neighbour across face f, with the same margin. `bead_pos`: beads lie in their device's region with the same margin; bonded live beads are 0.88 to 1.13 apart and no two live beads are closer than 0.88. `bead_chains`: some device holds 32 chains. `bond_list`: a live bond joins two live slots of its device.
All inputs are finite; a program needn't handle non-finite values.
Results may differ from a plain program's by a relative error of at most 0.0003.
Values sent between devices are 32-bit elements; how exact they have to be, the bound alone decides.
A program may use at most 128 MiB of HBM per device.

v0:
```python
import math

import jax
import jax.numpy as jnp
from jax import lax
from jax.sharding import PartitionSpec as P

UNITS = 16
NAXES = 32
CHAIN = 8


bead_mass = 5.0
step_size = 0.02
spring = 30.0
reach_square = 2.25
far_point = -1000.0
cut_square = 2.0 ** (1.0 / 3.0)
turn_cosine = math.cos(130.0 * math.pi / 180.0)
turn_sine = math.sin(130.0 * math.pi / 180.0)
golden = math.pi * (3.0 - math.sqrt(5.0))
block_rows = 1024


def with_halo(value, sides, width):
    edges = {}
    for axis, dim in sides:
        peers, length = (lax.axis_size(axis), value.shape[dim])
        up = [(i, (i + 1) % peers) for i in range(peers)]
        last = lax.slice_in_dim(value, length - width, length, axis=dim)
        first = lax.slice_in_dim(value, 0, width, axis=dim)
        edges[dim] = (
            lax.ppermute(last, axis, up),
            lax.ppermute(first, axis, [(b, a) for a, b in up]),
        )
    done = []
    for _, dim in sides:
        low, high = edges[dim]
        around = [(width, width) if d in done else (0, 0) for d in range(value.ndim)]
        value = jnp.concatenate([jnp.pad(low, around), value, jnp.pad(high, around)], axis=dim)
        done.append(dim)
    return value


def shifted(value, axis, by):
    peers = lax.axis_size(axis)
    return lax.ppermute(value, axis, [(i, (i + by) % peers) for i in range(peers)])


def with_halo_2(value, sides, width):
    for axis, dim in sides:
        peers, length = (lax.axis_size(axis), value.shape[dim])
        up = [(i, (i + 1) % peers) for i in range(peers)]
        down = [(j, i) for i, j in up]
        last = lax.slice_in_dim(value, length - width, length, axis=dim)
        first = lax.slice_in_dim(value, 0, width, axis=dim)
        before = lax.ppermute(last, axis, up)
        after = lax.ppermute(first, axis, down)
        value = jnp.concatenate([before, value, after], axis=dim)
    return value


def axis_table():
    counter = jnp.arange(NAXES).astype(jnp.float32)
    height = 1.0 - (2.0 * counter + 1.0) / NAXES
    radius = jnp.sqrt(1.0 - height * height)
    return jnp.stack(
        [radius * jnp.cos(golden * counter), radius * jnp.sin(golden * counter), height]
    )


def axis_vectors(indices):
    directions = axis_table()
    one_hot = (indices.reshape(1, -1) == jnp.arange(NAXES, dtype=jnp.int32)[:, None]).astype(
        jnp.float32
    )
    return jnp.dot(directions, one_hot, precision=lax.Precision.HIGHEST).reshape(
        (3,) + indices.shape
    )


def rotate(relative, normal):
    along_axis = jnp.sum(normal * relative, axis=0, keepdims=True)
    crossed = jnp.stack(
        [
            normal[1] * relative[2] - normal[2] * relative[1],
            normal[2] * relative[0] - normal[0] * relative[2],
            normal[0] * relative[1] - normal[1] * relative[0],
        ]
    )
    return turn_cosine * relative + turn_sine * crossed + (1.0 - turn_cosine) * along_axis * normal


def pair_force(own_rows, ghost_rows):

    def pair_add_block(running, ghost_block):
        differ = own_rows[:, :, None] - ghost_block[:, None, :]
        square = jnp.sum(differ * differ, axis=0)
        inside = (square < cut_square) & (square > 0.25)
        inverse = 1.0 / jnp.where(inside, square, 1.0)
        sixth_power = inverse * inverse * inverse
        weight = jnp.where(
            inside, 24.0 * (2.0 * sixth_power * sixth_power - sixth_power) * inverse, 0.0
        )
        return (running + jnp.sum(weight[None] * differ, axis=2), None)

    running, unused = lax.scan(pair_add_block, jnp.zeros_like(own_rows), ghost_rows)
    return running


def bond_force(own_rows, bond_pairs, bond_live):
    slot_ids = jnp.arange(own_rows.shape[1], dtype=jnp.int32)
    first_hot = (bond_pairs[0][:, None] == slot_ids[None]).astype(jnp.float32)
    second_hot = (bond_pairs[1][:, None] == slot_ids[None]).astype(jnp.float32)
    differ = lax.dot_general(
        own_rows, first_hot - second_hot, (((1,), (1,)), ((), ())), precision=lax.Precision.HIGHEST
    )
    square = jnp.sum(differ * differ, axis=0)
    weight = jnp.where(bond_live, -spring / (1.0 - square / reach_square), 0.0)
    pulling = weight[None] * differ
    return jnp.dot(pulling, first_hot, precision=lax.Precision.HIGHEST) - jnp.dot(
        pulling, second_hot, precision=lax.Precision.HIGHEST
    )


def cell_tables(plane_id, depth_id, planes, depths):
    plane_hot = (jnp.arange(planes, dtype=jnp.int32)[:, None] == plane_id[None]).astype(jnp.float32)
    depth_hot = (jnp.arange(depths, dtype=jnp.int32)[:, None] == depth_id[None]).astype(jnp.float32)
    return (plane_hot, depth_hot)


def binned_sums(moments, plane_id, depth_id, planes, depths):
    count = moments.shape[1]
    blocks = (count + block_rows - 1) // block_rows
    padding = blocks * block_rows - count
    moment_blocks = (
        jnp.pad(moments, ((0, 0), (0, padding))).reshape(4, blocks, block_rows).transpose(1, 0, 2)
    )
    plane_blocks = jnp.pad(plane_id, (0, padding), constant_values=-1).reshape(blocks, block_rows)
    depth_blocks = jnp.pad(depth_id, (0, padding), constant_values=-1).reshape(blocks, block_rows)

    def binned_add_block(running, pieces):
        moment_piece, plane_piece, depth_piece = pieces
        plane_hot, depth_hot = cell_tables(plane_piece, depth_piece, planes, depths)
        spread = (moment_piece[:, None, :] * depth_hot[None]).reshape(4 * depths, block_rows)
        return (
            running
            + lax.dot_general(
                spread, plane_hot, (((1,), (1,)), ((), ())), precision=lax.Precision.HIGHEST
            ),
            None,
        )

    start = jnp.zeros((4 * depths, planes), jnp.float32)
    totals, unused = lax.scan(binned_add_block, start, (moment_blocks, plane_blocks, depth_blocks))
    return totals.reshape(4, depths, planes).transpose(0, 2, 1)


def binned_lookup(cell_info, plane_id, depth_id, planes, depths):
    count = plane_id.shape[0]
    channels = cell_info.shape[0]
    blocks = (count + block_rows - 1) // block_rows
    padding = blocks * block_rows - count
    plane_blocks = jnp.pad(plane_id, (0, padding)).reshape(blocks, block_rows)
    depth_blocks = jnp.pad(depth_id, (0, padding)).reshape(blocks, block_rows)
    table = (
        cell_info.reshape(channels, planes, depths)
        .transpose(0, 2, 1)
        .reshape(channels * depths, planes)
    )

    def read_block(pieces):
        plane_piece, depth_piece = pieces
        plane_hot, depth_hot = cell_tables(plane_piece, depth_piece, planes, depths)
        rows = jnp.dot(table, plane_hot, precision=lax.Precision.HIGHEST).reshape(
            channels, depths, block_rows
        )
        return jnp.sum(rows * depth_hot[None], axis=1)

    picked = lax.map(read_block, (plane_blocks, depth_blocks))
    return picked.transpose(1, 0, 2).reshape(channels, blocks * block_rows)[:, :count]


def shards(
    sol_pos,
    sol_vel,
    sol_rows,
    mig_pos,
    mig_vel,
    mig_rows,
    bead_pos,
    bead_vel,
    bead_chains,
    bond_list,
    cell_axis,
    shift,
):
    size_x, size_y, size_z = cell_axis.shape
    slots_here = sol_pos.shape[-1]
    buffer_slots = mig_pos.shape[-1]
    bead_slots = bead_pos.shape[-1]
    bond_slots = bond_list.shape[-1]
    devices_x = lax.axis_size("gx")
    devices_y = lax.axis_size("gy")
    devices_z = lax.axis_size("gz")
    index_x = lax.axis_index("gx")
    index_y = lax.axis_index("gy")
    index_z = lax.axis_index("gz")
    face_live = jnp.arange(buffer_slots, dtype=jnp.int32)[None] < 128 * mig_rows.reshape(6, 1)
    packed = jnp.concatenate([mig_pos, mig_vel], axis=0)
    filler = jnp.array([far_point, far_point, far_point, 0.0, 0.0, 0.0], jnp.float32).reshape(
        6, 1, 1, 1, 1, 1
    )
    packed = jnp.where(face_live.reshape(1, 1, 1, 1, 6, buffer_slots), packed, filler)
    widened = with_halo(packed, (("gx", 1), ("gy", 2), ("gz", 3)), 1)
    pieces = [
        widened[:, 0, 1, 1, 1],
        widened[:, 2, 1, 1, 0],
        widened[:, 1, 0, 1, 3],
        widened[:, 1, 2, 1, 2],
        widened[:, 1, 1, 0, 5],
        widened[:, 1, 1, 2, 4],
    ]
    arriving = jnp.concatenate([received for received in pieces], axis=1)
    resident_live = jnp.arange(slots_here, dtype=jnp.int32) < 128 * sol_rows.reshape(())
    solvent_live = jnp.concatenate([resident_live, arriving[0] > -500.0])
    solvent_pos = jnp.concatenate([sol_pos.reshape(3, slots_here), arriving[:3]], axis=1)
    solvent_vel = jnp.concatenate([sol_vel.reshape(3, slots_here), arriving[3:]], axis=1)
    chains_here = bead_chains.reshape(())
    bead_live = jnp.arange(bead_slots, dtype=jnp.int32) < CHAIN * chains_here
    bond_live = jnp.arange(bond_slots, dtype=jnp.int32) < (CHAIN - 1) * chains_here
    bond_pairs = bond_list.reshape(2, bond_slots)
    bead_start = bead_pos.reshape(3, bead_slots)
    anchor = jnp.stack([index_x * size_x, index_y * size_y, index_z * size_z])
    position = jnp.concatenate([solvent_pos, bead_start], axis=1)
    velocity = jnp.concatenate([solvent_vel, bead_vel.reshape(3, bead_slots)], axis=1)
    all_live = jnp.concatenate([solvent_live, bead_live])
    weight = jnp.concatenate(
        [solvent_live.astype(jnp.float32), bead_mass * bead_live.astype(jnp.float32)]
    )
    levels = (
        jnp.floor(position * UNITS + shift.astype(jnp.float32)[:, None]).astype(jnp.int32) // UNITS
        - anchor[:, None]
    )
    planes = (size_x + 1) * (size_y + 1)
    depths = size_z + 1
    plane_id = jnp.where(all_live, levels[0] * (size_y + 1) + levels[1], 0)
    depth_id = jnp.where(all_live, levels[2], 0)
    moments = jnp.concatenate([weight[None], weight[None] * velocity], axis=0)
    moment_sums = binned_sums(moments, plane_id, depth_id, planes, depths)
    moment_sums = moment_sums.reshape(4, size_x + 1, size_y + 1, size_z + 1)
    received = shifted(moment_sums[:, size_x:], "gx", 1)
    moment_sums = moment_sums[:, :size_x] + jnp.concatenate(
        [received, jnp.zeros_like(moment_sums[:, 1:size_x])], axis=1
    )
    received = shifted(moment_sums[:, :, size_y:], "gy", 1)
    moment_sums = moment_sums[:, :, :size_y] + jnp.concatenate(
        [received, jnp.zeros_like(moment_sums[:, :, 1:size_y])], axis=2
    )
    received = shifted(moment_sums[:, :, :, size_z:], "gz", 1)
    moment_sums = moment_sums[:, :, :, :size_z] + jnp.concatenate(
        [received, jnp.zeros_like(moment_sums[:, :, :, 1:size_z])], axis=3
    )
    cell_info = jnp.concatenate(
        [moment_sums[1:] / jnp.maximum(moment_sums[:1], 1.0), axis_vectors(cell_axis)], axis=0
    )
    cell_info = jnp.concatenate([cell_info, shifted(cell_info[:, :, :, :1], "gz", -1)], axis=3)
    cell_info = jnp.concatenate([cell_info, shifted(cell_info[:, :, :1], "gy", -1)], axis=2)
    cell_info = jnp.concatenate([cell_info, shifted(cell_info[:, :1], "gx", -1)], axis=1)
    picked = binned_lookup(
        cell_info.reshape(6, planes * depths), plane_id, depth_id, planes, depths
    )
    local_flow = picked[:3]
    collided = local_flow + rotate(velocity - local_flow, picked[3:])
    count_solvent = solvent_pos.shape[1]
    sol_new = collided[:, :count_solvent]
    bead_new = collided[:, count_solvent:]
    sol_vel_out = jnp.where(solvent_live[None], sol_new, 0.0)
    cell_offset = solvent_pos - jnp.floor(solvent_pos) - 0.5
    sol_pos_out = jnp.where(solvent_live[None], cell_offset + 3.0 * step_size * sol_new, 0.0)
    offsets = jnp.arange(3, dtype=jnp.int32) - 1
    wrap_x = (index_x + offsets) // devices_x
    wrap_y = (index_y + offsets) // devices_y
    wrap_z = (index_z + offsets) // devices_z
    image_shift = jnp.stack(
        jnp.broadcast_arrays(
            size_x * devices_x * wrap_x[:, None, None],
            size_y * devices_y * wrap_y[None, :, None],
            size_z * devices_z * wrap_z[None, None, :],
        )
    ).astype(jnp.float32)[..., None]

    def forces(bead_at):
        placed = jnp.where(bead_live[None], bead_at, far_point)
        ghosts = with_halo_2(
            placed.reshape(3, 1, 1, 1, bead_slots), (("gx", 1), ("gy", 2), ("gz", 3)), 1
        )
        ghosts = (ghosts + image_shift).reshape(3, 27, bead_slots).transpose(1, 0, 2)
        return pair_force(placed, ghosts) + bond_force(placed, bond_pairs, bond_live)

    half_kick = 0.5 * step_size / bead_mass
    moved = jnp.zeros_like(bead_start)
    bead_speed = bead_new
    pushes = forces(bead_start)
    for substep in range(3):
        bead_speed = bead_speed + half_kick * pushes
        moved = moved + step_size * bead_speed
        pushes = forces(bead_start + moved)
        bead_speed = bead_speed + half_kick * pushes
    bead_pos_out = jnp.where(bead_live[None], moved, 0.0)
    bead_vel_out = jnp.where(bead_live[None], bead_speed, 0.0)
    return (
        sol_pos_out.reshape(3, 1, 1, 1, count_solvent),
        sol_vel_out.reshape(3, 1, 1, 1, count_solvent),
        bead_pos_out.reshape(3, 1, 1, 1, bead_slots),
        bead_vel_out.reshape(3, 1, 1, 1, bead_slots),
    )


def solution(mesh):
    return jax.shard_map(
        shards,
        mesh=mesh,
        in_specs=(
            P(None, "gx", "gy", "gz", None),
            P(None, "gx", "gy", "gz", None),
            P("gx", "gy", "gz"),
            P(None, "gx", "gy", "gz", None, None),
            P(None, "gx", "gy", "gz", None, None),
            P("gx", "gy", "gz", None),
            P(None, "gx", "gy", "gz", None),
            P(None, "gx", "gy", "gz", None),
            P("gx", "gy", "gz"),
            P(None, "gx", "gy", "gz", None),
            P("gx", "gy", "gz"),
            P(),
        ),
        out_specs=(
            P(None, "gx", "gy", "gz", None),
            P(None, "gx", "gy", "gz", None),
            P(None, "gx", "gy", "gz", None),
            P(None, "gx", "gy", "gz", None),
        ),
        check_vma=False,
    )
```

profile of v0, /device:TPU:0, one launch (start us, length us, event | category | flops | bytes accessed | tf_op | source)
XLA Modules:
  0.0 592.2 jit_solution(3841178530366969384)
XLA Ops:
  1.5 1.6 broadcast_select_fusion
  3.1 1.7 collective-permute-start
  4.7 2.7 collective-permute-start.1
  7.4 3.0 collective-permute-start.3
  10.4 3.8 collective-permute-start.4
  23.3 4.4 collective-permute-start.13
  29.5 1.0 collective-permute-done.4
  31.3 8.4 %collective-permute-done.5 = f32[6,1,1,1,6,3072]{5,3,4,2,1,0:T(1,128)S(1)} collective-permute-done((f32[6,1,1,1,6,3072]{5,3,4,2,1,0:T(1,128)S(1)}, f32[6,1,1,1,6,3072]{5,3,4,2,1,0:T(1,128)S(1)}, u32[]{:S(2)}, u32[]{:S(2)}) %collective-permute-start.5) | collective-permute-done | bytes 442400 | tf_op jit(solution)/shard_map/ppermute | solution.py:34
  40.1 1.7 fusion.39
  41.9 1.7 slice_reduce_fusion
  47.1 1.8 reshape.443
  48.9 190.1 %while.66 = (s32[]{:T(128)}, f32[132,289]{1,0:T(8,128)S(1)}, f32[67,4,1024]{2,0,1:T(8,128)}, s32[67,1024]{1,0:T(8,128)S(1)}, s32[67,1024]{1,0:T(8,128)}, /*index=5*/s32[]{:T(128)}, s32[]{:T(128)}) while((s32[]{:T(128)}, f32[132,289]{1,0:T(8,128)S(1)}, f32[67,4,1024]{2,0,1:T(8,128)}, s32[67,1024]{1,0:T(8,128)S(1)}, ...), condition=%wide.region_1.2_spmd.clone, body=%wide.region_0.1_spmd.clone.sunk | while | flops 469337600 | bytes 2844799 | solution.py:155
  50.8 0.9 fusion.140
  56.5 0.9 fusion.140
  62.2 0.9 fusion.140
  73.5 0.9 fusion.140
  170.0 0.9 fusion.140
  181.3 0.9 fusion.140
  240.3 5.2 collective-permute-done.6
  245.7 1.7 collective-permute-start.14
  247.4 1.3 collective-permute-start.15
  248.7 1.5 collective-permute-done.7
  251.0 3.3 collective-permute-start.16
  254.6 10.2 %collective-permute-done.8 = f32[4,16,16,1]{3,0,2,1:T(4,128)S(1)} collective-permute-done((f32[4,16,16,1]{3,0,2,1:T(4,128)S(1)}, f32[4,16,16,1]{3,0,2,1:T(4,128)S(1)}, u32[]{:S(2)}, u32[]{:S(2)}) %collective-permute-start.8) | collective-permute-done | bytes 4128 | tf_op jit(solution)/shard_map/ppermute | solution.py:47
  266.7 5.3 collective-permute-done.9
  272.0 1.4 copy.70
  273.6 1.8 collective-permute-done.10
  275.5 1.4 collective-permute-start.11
  277.0 17.8 %while.67 = (s32[]{:T(128)}, f32[3,256]{1,0:T(4,128)S(1)}, f32[3,256]{1,0:T(4,128)S(1)}, f32[27,3,256]{2,1,0:T(4,128)S(1)}, s32[]{:T(128)}, /*index=5*/s32[]{:T(128)}) while((s32[]{:T(128)}, f32[3,256]{1,0:T(4,128)S(1)}, f32[3,256]{1,0:T(4,128)S(1)}, f32[27,3,256]{2,1,0:T(4,128)S(1)}, s32[]{:T(128)}, /*index=5*/s32[]{:T(128)}) %tuple.160), condition=%wide.region_9.10_spmd.clone, body=%wide.region_6.9_spmd.clone.sunk | while | flops 1966851 | bytes 1079379 | solution.py:107
  294.7 1.7 reshape.440
  296.4 1.7 reshape.450
  298.1 2.3 pad_maximum_fusion
  300.5 1.6 reshape.459
  302.2 174.8 %while.65 = (s32[]{:T(128)}, f32[67,6,1024]{2,1,0:T(8,128)}, s32[67,1024]{1,0:T(8,128)}, f32[198,289]{1,0:T(8,128)S(1)}, s32[67,1024]{1,0:T(8,128)}, /*index=5*/s32[]{:T(128)}) while((s32[]{:T(128)}, f32[67,6,1024]{2,1,0:T(8,128)}, s32[67,1024]{1,0:T(8,128)}, f32[198,289]{1,0:T(8,128)S(1)}, s32[67,1024]{1,0:T(8,128)}, ...), condition=%wide.region_4.5_spmd, body=%wide.region_2.4_spmd.sunk | while | flops 703906816 | bytes 3850337 | solution.py:180
  477.0 3.7 multiply_reduce_fusion.1
  480.7 1.4 multiply_subtract_fusion.6
  482.2 1.4 fusion.45
  483.9 1.0 collective-permute-start.18
  484.9 3.3 collective-permute-start.19
  490.3 2.4 collective-permute-start.21
  492.7 1.4 collective-permute-done.20
  494.1 1.2 collective-permute-start.22
  495.3 2.4 collective-permute-start.23
  497.9 1.8 copy.75
  499.7 1.7 copy.76
  501.5 17.8 %while.68 = (s32[]{:T(128)}, f32[3,256]{1,0:T(4,128)S(1)}, f32[3,256]{1,0:T(4,128)S(1)}, f32[27,3,256]{2,1,0:T(4,128)S(1)}, s32[]{:T(128)}, /*index=5*/s32[]{:T(128)}) while((s32[]{:T(128)}, f32[3,256]{1,0:T(4,128)S(1)}, f32[3,256]{1,0:T(4,128)S(1)}, f32[27,3,256]{2,1,0:T(4,128)S(1)}, s32[]{:T(128)}, ...), condition=%wide.region_14.15_spmd.clone, body=%wide.region_11.14_spmd.clone.sunk | while | flops 1966851 | bytes 1079379 | solution.py:107
  519.7 4.2 collective-permute-start.25
  524.2 1.1 collective-permute-done.24
  525.4 2.9 collective-permute-start.27
  528.4 1.4 collective-permute-done.26
  529.8 2.4 collective-permute-start.28
  532.2 1.2 collective-permute-start.29
  533.6 1.7 collective-permute-done.28
  535.3 2.4 collective-permute-done.29
  537.8 17.8 %while.69 = (s32[]{:T(128)}, f32[3,256]{1,0:T(4,128)S(1)}, f32[3,256]{1,0:T(4,128)S(1)}, f32[27,3,256]{2,1,0:T(4,128)S(1)}, s32[]{:T(128)}, /*index=5*/s32[]{:T(128)}) while((s32[]{:T(128)}, f32[3,256]{1,0:T(4,128)S(1)}, f32[3,256]{1,0:T(4,128)S(1)}, f32[27,3,256]{2,1,0:T(4,128)S(1)}, s32[]{:T(128)}, ...), condition=%wide.region_19.20_spmd.clone, body=%wide.region_16.19_spmd.clone.sunk | while | flops 1966851 | bytes 1079379 | solution.py:107
  556.3 3.7 collective-permute-start.31
  560.4 1.2 collective-permute-done.30
  561.7 2.9 collective-permute-start.33
  564.6 1.4 collective-permute-done.32
  566.0 1.9 collective-permute-start.34
  568.0 1.7 collective-permute-start.35
  570.5 1.1 collective-permute-done.34
  571.6 1.8 collective-permute-done.35
  573.6 17.8 %while.70 = (s32[]{:T(128)}, f32[3,256]{1,0:T(4,128)S(1)}, f32[3,256]{1,0:T(4,128)S(1)}, f32[27,3,256]{2,1,0:T(4,128)S(1)}, s32[]{:T(128)}, /*index=5*/s32[]{:T(128)}) while((s32[]{:T(128)}, f32[3,256]{1,0:T(4,128)S(1)}, f32[3,256]{1,0:T(4,128)S(1)}, f32[27,3,256]{2,1,0:T(4,128)S(1)}, s32[]{:T(128)}, ...), condition=%wide.region_24.25_spmd.clone, body=%wide.region_21.24_spmd.clone.sunk | while | flops 1966851 | bytes 1079379 | solution.py:107
  (1600 shorter events, 445.9 us)
Async XLA Ops:
  0.6 14.9 %copy-start.4 = (f32[3,1,1,1,49152]{4,3,2,1,0:T(1,128)S(1)}, f32[3,1,1,1,49152]{4,3,2,1,0:T(1,128)}, u32[]{:S(2)}) copy-start(f32[3,1,1,1,49152]{4,3,2,1,0:T(1,128)} %param.25) | copy-start | bytes 1769476
  1.4 14.6 %copy-start.8 = (f32[3,1,1,1,256]{4,3,2,1,0:T(1,128)S(1)}, f32[3,1,1,1,256]{4,3,2,1,0:T(1,128)}, u32[]{:S(2)}) copy-start(f32[3,1,1,1,256]{4,3,2,1,0:T(1,128)} %param.31) | copy-start | bytes 9220
  1.5 14.6 %copy-start.20 = (s32[3]{0:T(128)S(1)}, s32[3]{0:T(128)}, u32[]{:S(2)}) copy-start(s32[3]{0:T(128)} %param.36) | copy-start | bytes 40
  1.5 15.3 %copy-start.5 = (f32[3,1,1,1,49152]{4,3,2,1,0:T(1,128)S(1)}, f32[3,1,1,1,49152]{4,3,2,1,0:T(1,128)}, u32[]{:S(2)}) copy-start(f32[3,1,1,1,49152]{4,3,2,1,0:T(1,128)} %param.26) | copy-start | bytes 1769476
  3.1 17.6 %collective-permute-start = (f32[6,1,1,1,6,3072]{5,3,4,2,1,0:T(1,128)S(1)}, f32[6,1,1,1,6,3072]{5,3,4,2,1,0:T(1,128)}, u32[]{:S(2)}, u32[]{:S(2)}) collective-permute-start(f32[6,1,1,1,6,3072]{5,3,4,2,1,0:T(1,128)S(1)} %broadcast_select_fusion), channel_id=1, source_target_pairs={{0,16},{16,32},{32,48},{48,64},{64,80},{80,96},{96,112},{112,0},{1... | collective-permute-start | bytes 1327112 | tf_op jit(solution)/shard_map/ppermute | solution.py:33
  4.7 17.5 %collective-permute-start.1 = (f32[6,1,1,1,6,3072]{5,3,4,2,1,0:T(1,128)S(1)}, f32[6,1,1,1,6,3072]{5,3,4,2,1,0:T(1,128)}, u32[]{:S(2)}, u32[]{:S(2)}) collective-permute-start(f32[6,1,1,1,6,3072]{5,3,4,2,1,0:T(1,128)S(1)} %broadcast_select_fusion), channel_id=1, source_target_pairs={{16,0},{32,16},{48,32},{64,48},{80,64},{96,80},{112,96},{0,112},{1... | collective-permute-start | bytes 1327112 | tf_op jit(solution)/shard_map/ppermute | solution.py:34
  7.4 15.8 %collective-permute-start.2 = (f32[6,1,1,1,6,3072]{5,3,4,2,1,0:T(1,128)S(1)}, f32[6,1,1,1,6,3072]{5,3,4,2,1,0:T(1,128)}, u32[]{:S(2)}, u32[]{:S(2)}) collective-permute-start(f32[6,1,1,1,6,3072]{5,3,4,2,1,0:T(1,128)S(1)} %broadcast_select_fusion), channel_id=1, source_target_pairs={{0,2},{2,4},{4,6},{6,8},{8,10},{10,12},{12,14},{14,0},{1,3},{3,5},... | collective-permute-start | bytes 1327112 | tf_op jit(solution)/shard_map/ppermute | solution.py:33
  7.4 21.1 %collective-permute-start.3 = (f32[6,1,1,1,6,3072]{5,3,4,2,1,0:T(1,128)S(1)}, f32[6,1,1,1,6,3072]{5,3,4,2,1,0:T(1,128)}, u32[]{:S(2)}, u32[]{:S(2)}) collective-permute-start(f32[6,1,1,1,6,3072]{5,3,4,2,1,0:T(1,128)S(1)} %broadcast_select_fusion), channel_id=1, source_target_pairs={{2,0},{4,2},{6,4},{8,6},{10,8},{12,10},{14,12},{0,14},{3,1},{5,3},... | collective-permute-start | bytes 1327112 | tf_op jit(solution)/shard_map/ppermute | solution.py:34
  10.4 20.1 %collective-permute-start.4 = (f32[6,1,1,1,6,3072]{5,3,4,2,1,0:T(1,128)S(1)}, f32[6,1,1,1,6,3072]{5,3,4,2,1,0:T(1,128)}, u32[]{:S(2)}, u32[]{:S(2)}) collective-permute-start(f32[6,1,1,1,6,3072]{5,3,4,2,1,0:T(1,128)S(1)} %broadcast_select_fusion), channel_id=1, source_target_pairs={{0,1},{1,0},{2,3},{3,2},{4,5},{5,4},{6,7},{7,6},{8,9},{9,8},{10,11... | collective-permute-start | bytes 1327112 | tf_op jit(solution)/shard_map/ppermute | solution.py:33
  15.6 1.6 copy-start.9
  15.6 1.6 copy-start.7
  16.0 2.8 copy-start.10
  17.2 29.0 %copy-start.1 = (f32[3,1,1,1,49152]{4,0,2,1,3:T(4,128)}, f32[3,1,1,1,49152]{4,0,2,1,3:T(4,128)S(1)}, u32[]{:S(2)}) copy-start(f32[3,1,1,1,49152]{4,0,2,1,3:T(4,128)S(1)} %copy.129) | copy-start | bytes 1769476
  18.8 1.3 copy-start.18
  18.8 4.4 copy-start.16
  19.2 22.6 %copy-start.21 = (f32[3,224]{1,0:T(4,128)}, f32[3,224]{1,0:T(4,128)S(1)}, u32[]{:S(2)}) copy-start(f32[3,224]{1,0:T(4,128)S(1)} %get-tuple-element.341) | copy-start | bytes 8068
  19.3 0.9 copy-start.14
  20.7 19.1 %collective-permute-start.5 = (f32[6,1,1,1,6,3072]{5,3,4,2,1,0:T(1,128)S(1)}, f32[6,1,1,1,6,3072]{5,3,4,2,1,0:T(1,128)S(1)}, u32[]{:S(2)}, u32[]{:S(2)}) collective-permute-start(f32[6,1,1,1,6,3072]{5,3,4,2,1,0:T(1,128)S(1)} %broadcast_select_fusion), channel_id=1, source_target_pairs={{1,0},{0,1},{3,2},{2,3},{5,4},{4,5},{7,6},{6,7},{9,8},{8,9},{11,10... | collective-permute-start | bytes 1327112 | tf_op jit(solution)/shard_map/ppermute | solution.py:34
  22.3 223.4 %collective-permute-start.12 = (f32[3,1,1,1,256]{4,3,2,1,0:T(1,128)S(1)}, f32[3,1,1,1,256]{4,3,2,1,0:T(1,128)S(1)}, u32[]{:S(2)}, u32[]{:S(2)}) collective-permute-start(f32[3,1,1,1,256]{4,3,2,1,0:T(1,128)S(1)} %broadcast_select_fusion.3), channel_id=1, source_target_pairs={{0,16},{16,32},{32,48},{48,64},{64,80},{80,96},{96,112},{112,0},{1... | collective-permute-start | bytes 9224 | tf_op jit(solution)/shard_map/ppermute | solution.py:57
  23.3 222.4 %collective-permute-start.13 = (f32[3,1,1,1,256]{4,3,2,1,0:T(1,128)S(1)}, f32[3,1,1,1,256]{4,3,2,1,0:T(1,128)S(1)}, u32[]{:S(2)}, u32[]{:S(2)}) collective-permute-start(f32[3,1,1,1,256]{4,3,2,1,0:T(1,128)S(1)} %broadcast_select_fusion.3), channel_id=1, source_target_pairs={{16,0},{32,16},{48,32},{64,48},{80,64},{96,80},{112,96},{0,112},{1... | collective-permute-start | bytes 9224 | tf_op jit(solution)/shard_map/ppermute | solution.py:58
  39.9 2.0 copy-start.2
  44.3 1.7 copy-start.13
  239.1 0.7 copy-start.11
  239.1 0.7 copy-start.12
  239.5 6.1 %collective-permute-start.6 = (f32[4,1,17,33]{3,0,2,1:T(4,128)S(1)}, f32[4,1,17,33]{3,0,2,1:T(4,128)S(1)}, u32[]{:S(2)}, u32[]{:S(2)}) collective-permute-start(f32[4,1,17,33]{3,0,2,1:T(4,128)S(1)} %slice.177), channel_id=1, source_target_pairs={{0,16},{16,32},{32,48},{48,64},{64,80},{80,96},{96,112},{112,0},{1... | collective-permute-start | bytes 26936 | tf_op jit(solution)/shard_map/ppermute | solution.py:47
  245.6 4.6 collective-permute-start.7
  245.7 5.2 collective-permute-start.14
  247.4 3.6 collective-permute-start.15
  250.6 14.2 %collective-permute-start.8 = (f32[4,16,16,1]{3,0,2,1:T(4,128)S(1)}, f32[4,16,16,1]{3,0,2,1:T(4,128)S(1)}, u32[]{:S(2)}, u32[]{:S(2)}) collective-permute-start(f32[4,16,16,1]{3,0,2,1:T(4,128)S(1)} %slice.181), channel_id=1, source_target_pairs={{0,1},{1,0},{2,3},{3,2},{4,5},{5,4},{6,7},{7,6},{8,9},{9,8},{10,11... | collective-permute-start | bytes 12296 | tf_op jit(solution)/shard_map/ppermute | solution.py:47
  251.0 15.6 %collective-permute-start.16 = (f32[3,3,3,1,256]{4,3,2,1,0:T(1,128)S(1)}, f32[3,3,3,1,256]{4,3,2,1,0:T(1,128)S(1)}, u32[]{:S(2)}, u32[]{:S(2)}) collective-permute-start(f32[3,3,3,1,256]{4,3,2,1,0:T(1,128)S(1)} %pad_maximum_fusion.16), channel_id=1, source_target_pairs={{0,1},{1,0},{2,3},{3,2},{4,5},{5,4},{6,7},{7,6},{8,9},{9,8},{10,11... | collective-permute-start | bytes 82952 | tf_op jit(solution)/shard_map/ppermute | solution.py:57
  254.3 12.3 %collective-permute-start.17 = (f32[3,3,3,1,256]{4,3,2,1,0:T(1,128)S(1)}, f32[3,3,3,1,256]{4,3,2,1,0:T(1,128)S(1)}, u32[]{:S(2)}, u32[]{:S(2)}) collective-permute-start(f32[3,3,3,1,256]{4,3,2,1,0:T(1,128)S(1)} %pad_maximum_fusion.16), channel_id=1, source_target_pairs={{1,0},{0,1},{3,2},{2,3},{5,4},{4,5},{7,6},{6,7},{9,8},{8,9},{11,10... | collective-permute-start | bytes 82952 | tf_op jit(solution)/shard_map/ppermute | solution.py:58
  266.2 5.7 collective-permute-start.9
  273.5 1.9 collective-permute-start.10
  275.5 22.6 %collective-permute-start.11 = (f32[6,1,17,33]{3,0,2,1:T(8,128)S(1)}, f32[6,1,17,33]{3,0,2,1:T(8,128)}, u32[]{:S(2)}, u32[]{:S(2)}) collective-permute-start(f32[6,1,17,33]{3,0,2,1:T(8,128)S(1)} %pad_maximum_fusion.8), channel_id=1, source_target_pairs={{0,112},{16,0},{32,16},{48,32},{64,48},{80,64},{96,80},{112,96},{1... | collective-permute-start | bytes 40400 | tf_op jit(solution)/shard_map/ppermute | solution.py:47
  477.0 3.7 copy-start
  482.2 1.4 copy-start.15
  482.2 1.4 copy-start.17
  482.2 1.4 copy-start.22
  482.2 1.4 copy-start.23
  482.2 5.9 copy-start.3
  482.2 5.9 copy-start.6
  483.9 5.8 collective-permute-start.18
  484.9 4.8 collective-permute-start.19
  488.1 0.8 copy-start.19
  489.7 4.3 collective-permute-start.20
  490.3 3.8 collective-permute-start.21
  494.1 7.3 %collective-permute-start.22 = (f32[3,3,3,1,256]{4,0,3,2,1:T(4,128)S(1)}, f32[3,3,3,1,256]{4,0,3,2,1:T(4,128)S(1)}, u32[]{:S(2)}, u32[]{:S(2)}) collective-permute-start(f32[3,3,3,1,256]{4,0,3,2,1:T(4,128)S(1)} %pad_maximum_fusion.13), channel_id=1, source_target_pairs={{0,1},{1,0},{2,3},{3,2},{4,5},{5,4},{6,7},{7,6},{8,9},{9,8},{10,11... | collective-permute-start | bytes 82952 | tf_op jit(solution)/shard_map/ppermute | solution.py:57
  495.3 6.1 %collective-permute-start.23 = (f32[3,3,3,1,256]{4,0,3,2,1:T(4,128)S(1)}, f32[3,3,3,1,256]{4,0,3,2,1:T(4,128)S(1)}, u32[]{:S(2)}, u32[]{:S(2)}) collective-permute-start(f32[3,3,3,1,256]{4,0,3,2,1:T(4,128)S(1)} %pad_maximum_fusion.13), channel_id=1, source_target_pairs={{1,0},{0,1},{3,2},{2,3},{5,4},{4,5},{7,6},{6,7},{9,8},{8,9},{11,10... | collective-permute-start | bytes 82952 | tf_op jit(solution)/shard_map/ppermute | solution.py:58
  519.6 5.8 collective-permute-start.24
  519.7 5.7 collective-permute-start.25
  525.4 4.3 collective-permute-start.26
  525.4 4.3 collective-permute-start.27
  529.8 5.5 collective-permute-start.28
  532.2 5.5 collective-permute-start.29
  555.9 5.8 collective-permute-start.30
  556.3 5.3 collective-permute-start.31
  561.7 4.3 collective-permute-start.32
  561.7 4.3 collective-permute-start.33
  566.0 5.5 collective-permute-start.34
  568.0 5.5 collective-permute-start.35
where the time goes:
time: 604 us; the launch traced here: 592 us
  local copies, waits for them, and re-layouts  245 us (41%)
  matrix products  128 us (21%)
  other arithmetic  101 us (17%)
  starting transfers between devices  57.5 us (10%)
  waiting for transfers between devices  47.3 us (8%)
  loops' own time  11 us (2%)
    dynamic_slice x268, local copies, waits for them, and re-layouts, binned_sums(): lax.scan(binned_add_block, start, (moment_blocks, plane_blocks, depth_blo...  167 us
    dot_general x67, matrix products, binned_add_block(): lax.dot_general(spread, plane_hot, (((1,), (1,)), ((), ())), precision=la...  62.6 us
    dot_general x67, matrix products, read_block(): jnp.dot(table, plane_hot, precision=lax.Precision.HIGHEST)  60.9 us
    dynamic_update_slice x67, local copies, waits for them, and re-layouts, binned_lookup(): picked = lax.map(read_block, (plane_blocks, depth_blocks))  41.5 us
    reduce_sum x108, other arithmetic, pair_add_block(): return (running + jnp.sum(weight[None] * differ, axis=2), None)  33.8 us
    ppermute x12, starting transfers between devices, with_halo_2(): after = lax.ppermute(first, axis, down)  30.6 us
    ppermute x6, waiting for transfers between devices, shifted(): lax.ppermute(value, axis, [(i, (i + by) % peers) for i in range(peers)])  24 us
    reduce_sum x108, other arithmetic, pair_add_block(): square = jnp.sum(differ * differ, axis=0)  18.2 us
  transfers between devices with their start and end apart: 36, of which 17 were waited for; matrix products, arithmetic and copies ran while one was open for 40% of the time, Pallas kernels for 0%

commit v1 on v0

v1 whole, which is shorter than its diff:
```python
import math

import jax
import jax.numpy as jnp
import numpy as np
from jax import lax
from jax.experimental import pallas as pl
from jax.experimental.pallas import tpu as pltpu
from jax.sharding import PartitionSpec as P

BF = jnp.bfloat16
F32 = jnp.float32
MESH = pl.DeviceIdType.MESH

UNITS = 16
NAXES = 32
CHAIN = 8
bead_mass = 5.0
step_size = 0.02
spring = 30.0
reach_square = 2.25
far_point = -1000.0
cut_square = 2.0 ** (1.0 / 3.0)
turn_cosine = math.cos(130.0 * math.pi / 180.0)
turn_sine = math.sin(130.0 * math.pi / 180.0)
golden = math.pi * (3.0 - math.sqrt(5.0))

LANES = 256
LEVELS = 38
CH = 8
TROWS = LEVELS * CH
RES = 384
FACE = 24
SOLV = RES + 6 * FACE
ALL = SOLV + 8
KR = 24
BEADS = 256
BONDS = 224

OFFSETS = [
    (dx, dy, dz)
    for dx in (-1, 0, 1)
    for dy in (-1, 0, 1)
    for dz in (0, 1)
    if (dx, dy, dz) != (0, 0, 0)
]
HALO = [(1, 0, 0), (0, 1, 0), (0, 0, 1), (1, 0, 1), (0, 1, 1), (1, 1, 0), (1, 1, 1)]


def slot(dx, dy, dz):
    return ((dx + 1) * 3 + dy + 1) * 2 + dz


def axis_rows():
    counter = np.arange(128) % NAXES
    height = 1.0 - (2.0 * counter + 1.0) / NAXES
    radius = np.sqrt(1.0 - height * height)
    rows = np.stack(
        [radius * np.cos(golden * counter), radius * np.sin(golden * counter), height]
    )
    return np.repeat(rows, 8, axis=0).astype(np.float32)


def split2(value):
    high = value.astype(BF).astype(F32)
    return high, (value - high).astype(BF).astype(F32)


def split3(value):
    high = value.astype(BF)
    rest = value - high.astype(F32)
    middle = rest.astype(BF)
    low = (rest - middle.astype(F32)).astype(BF)
    return high, middle, low


def nt(a, b):
    return lax.dot_general(a, b, (((1,), (1,)), ((), ())), preferred_element_type=F32)


def nn(a, b):
    return lax.dot_general(a, b, (((1,), (0,)), ((), ())), preferred_element_type=F32)


def rows_of(ref, row, count):
    return jnp.broadcast_to(ref[pl.ds(row, 1), :], (count, 128))


def rotated(v, u, n):
    w = [v[d] - u[d] for d in range(3)]
    along = (1.0 - turn_cosine) * (n[0] * w[0] + n[1] * w[1] + n[2] * w[2])
    crossed = [
        n[1] * w[2] - n[2] * w[1],
        n[2] * w[0] - n[0] * w[2],
        n[0] * w[1] - n[1] * w[0],
    ]
    return [u[d] + turn_cosine * w[d] + turn_sine * crossed[d] + along * n[d] for d in range(3)]


def kernel(
    sol_rows,
    mig_rows,
    chains,
    shift,
    sol_pos,
    sol_vel,
    mig_pos,
    mig_vel,
    bead_pos,
    bead_vel,
    bond_list,
    cell_axis,
    axis_tab,
    pos_out,
    vel_out,
    bpos_out,
    bvel_out,
    lo_s,
    hi_s,
    V_s,
    acc,
    iota_lo,
    iota_hi,
    arr_pos,
    arr_vel,
    arr_rows,
    row_send,
    bpack,
    mom,
    E_s,
    D_s,
    sx,
    sy,
    sz,
    se,
    rx,
    ry,
    rz,
    re,
    ux,
    uy,
    uz,
    ue,
    gx_,
    gy_,
    gz_,
    ge,
    U_s,
    T_f,
    T_s,
    psend,
    ghost,
    G_s,
    GT_s,
    F_s,
    W_s,
    mig_ss,
    mig_rs,
    halo_ss,
    halo_rs,
    info_ss,
    info_rs,
    bead_ss,
    bead_rs,
):
    ix = lax.axis_index("gx")
    iy = lax.axis_index("gy")
    iz = lax.axis_index("gz")

    def device(dx, dy, dz):
        return (
            lax.rem(ix + dx + 8, 8),
            lax.rem(iy + dy + 8, 8),
            lax.rem(iz + dz + 2, 2),
        )

    barrier = pltpu.get_barrier_semaphore()
    for off in OFFSETS:
        pl.semaphore_signal(barrier, inc=1, device_id=device(*off), device_id_type=MESH)

    iota_lo[...] = lax.broadcasted_iota(jnp.int32, (256, 128), 0).astype(F32).astype(BF)
    iota_hi[...] = (
        (lax.broadcasted_iota(jnp.int32, (TROWS, 128), 0) // CH).astype(F32).astype(BF)
    )
    acc[...] = jnp.zeros_like(acc)
    bpack[...] = jnp.zeros_like(bpack)
    one16 = jnp.ones((16, 128), BF)
    zero16 = jnp.zeros((16, 128), BF)
    sub8 = lax.broadcasted_iota(jnp.int32, (8, 128), 0)
    lane256 = lax.broadcasted_iota(jnp.int32, (1, 256), 1)
    anchor = [(ix * 16).astype(F32), (iy * 16).astype(F32), (iz * 32).astype(F32)]
    shifts = [shift[d].astype(F32) for d in range(3)]
    bead_live = lane256 < CHAIN * chains[0]
    bond_live = lane256 < (CHAIN - 1) * chains[0]

    start = [bead_pos[d] for d in range(3)]

    def place(exchange, value):
        for d in range(3):
            psend[exchange, d : d + 1, :] = jnp.where(bead_live, value[d], far_point)
        psend[exchange, 3:4, :] = jnp.zeros((1, 256), F32)

    place(0, start)
    for g in range(6):
        row_send[g] = jnp.broadcast_to(mig_rows[g], (1, 128)).astype(jnp.int32)

    def prep(row0, p, v, weight):
        level = []
        for d in range(3):
            level.append(jnp.floor((p[d] * 16.0 + shifts[d]) * 0.0625) - anchor[d])
        lx, ly, lz = level
        xe = lx > 15.5
        ye = ly > 15.5
        ze = lz > 31.5
        zb = jnp.where(lz > 15.5, 1.0, 0.0)
        zm = lz - 16.0 * zb
        both = xe & ye
        edge = xe | ye
        along = jnp.where(xe, ly, lx)
        lo_edge = jnp.where(
            both,
            32.0 + lz,
            jnp.where(ze, along + jnp.where(xe, 0.0, 16.0), along * 16.0 + zm),
        )
        hi_edge = jnp.where(both | ze, 37.0, jnp.where(xe, 33.0, 35.0) + zb)
        lo_s[pl.ds(row0, 8), :] = jnp.where(edge, lo_edge, lx * 16.0 + ly)
        hi_s[pl.ds(row0, 8), :] = jnp.where(edge, hi_edge, lz)
        V_s[pl.ds(row0 * 8, 8, stride=8), :] = weight
        for d in range(3):
            high, low = split2(weight * v[d])
            V_s[pl.ds(row0 * 8 + 1 + d, 8, stride=8), :] = high
            V_s[pl.ds(row0 * 8 + 4 + d, 8, stride=8), :] = low
        V_s[pl.ds(row0 * 8 + 7, 8, stride=8), :] = jnp.zeros((8, 128), F32)

    def resident_prep(b, carry):
        r = pl.multiple_of(b * 8, 8)
        weight = jnp.where(sub8 + r < sol_rows[0], 1.0, 0.0)
        prep(
            r,
            [sol_pos[d, pl.ds(r, 8), :] for d in range(3)],
            [sol_vel[d, pl.ds(r, 8), :] for d in range(3)],
            weight,
        )
        return carry

    lax.fori_loop(0, RES // 8, resident_prep, 0)

    row32 = lax.broadcasted_iota(jnp.int32, (32, 256), 0)
    col32 = lax.broadcasted_iota(jnp.int32, (32, 256), 1)
    mask_face = (col32 % 16) == (row32 % 16)
    mask_edge = (
        ((col32 < 32) & (row32 == 0))
        | ((col32 >= 32) & (col32 < 64) & (col32 - 32 == row32))
        | ((col32 == 64) & (row32 == 0))
    )
    er = lax.broadcasted_iota(jnp.int32, (256, 256), 0)
    ec = lax.broadcasted_iota(jnp.int32, (256, 256), 1)

    def as_bf(mask):
        return jnp.where(mask, 1.0, 0.0).astype(BF)

    E_s[0:256, :] = as_bf(ec == er // 16)
    E_s[256:512, :] = as_bf(ec == (er // 16) * 16)
    target = jnp.where(er < 16, er, jnp.where(er < 32, (er - 16) * 16, 0))
    E_s[512:768, :] = as_bf(ec == target)
    first = jnp.where(bond_live, bond_list[0], -1)
    second = jnp.where(bond_live, bond_list[1], -1)
    D_s[...] = (
        jnp.where(er == first, 1.0, 0.0) - jnp.where(er == second, 1.0, 0.0)
    ).astype(BF)

    pl.semaphore_wait(barrier, len(OFFSETS))

    faces = [(-1, 0, 0), (1, 0, 0), (0, -1, 0), (0, 1, 0), (0, 0, 1), (0, 0, 1)]

    def mig_copies(g, f):
        where = dict(device_id=device(*faces[g]), device_id_type=MESH)
        return [
            pltpu.make_async_remote_copy(
                src_ref=mig_pos.at[:, g],
                dst_ref=arr_pos.at[:, f],
                send_sem=mig_ss.at[0, g],
                recv_sem=mig_rs.at[0, f],
                **where,
            ),
            pltpu.make_async_remote_copy(
                src_ref=mig_vel.at[:, g],
                dst_ref=arr_vel.at[:, f],
                send_sem=mig_ss.at[1, g],
                recv_sem=mig_rs.at[1, f],
                **where,
            ),
            pltpu.make_async_remote_copy(
                src_ref=row_send.at[g],
                dst_ref=arr_rows.at[f],
                send_sem=mig_ss.at[2, g],
                recv_sem=mig_rs.at[2, f],
                **where,
            ),
        ]

    def bead_copy(exchange, off, into):
        return pltpu.make_async_remote_copy(
            src_ref=psend.at[exchange],
            dst_ref=ghost.at[exchange, into],
            send_sem=bead_ss.at[exchange, slot(*off)],
            recv_sem=bead_rs.at[exchange, into],
            device_id=device(*off),
            device_id_type=MESH,
        )

    def bead_send(exchange):
        for dx, dy, dz in OFFSETS:
            bead_copy(exchange, (dx, dy, dz), slot(-dx, -dy, dz)).start()

    def bead_arrive(exchange):
        for off in OFFSETS:
            bead_copy(exchange, off, slot(*off)).wait_recv()

    bead_send(0)
    for g in range(6):
        for copy in mig_copies(g, g ^ 1):
            copy.start()

    def hot_lo(row):
        lo_b = rows_of(lo_s, row, 16).astype(BF)
        return jnp.concatenate(
            [
                jnp.where(iota_lo[16 * j : 16 * j + 16, :] == lo_b, one16, zero16)
                for j in range(16)
            ],
            0,
        )

    def bin_rows(row0, count):
        spread = []
        hot = []
        for r in range(count):
            row = row0 + r
            hot.append(hot_lo(row))
            v = V_s[pl.ds(pl.multiple_of(row * 8, 8), 8), :]
            v = jnp.concatenate([v, v], 0).astype(BF)
            hi_b = rows_of(hi_s, row, 16).astype(BF)
            spread.append(
                jnp.concatenate(
                    [
                        jnp.where(iota_hi[16 * j : 16 * j + 16, :] == hi_b, v, zero16)
                        for j in range(TROWS // 16)
                    ],
                    0,
                )
            )
        sums = nt(jnp.concatenate(spread, 1), jnp.concatenate(hot, 1))
        acc[0:TROWS, :] += sums[:, 0:128]
        acc[TROWS : 2 * TROWS, :] += sums[:, 128:256]

    def bin_loop(b, carry):
        bin_rows(b * KR, KR)
        return carry

    lax.fori_loop(0, RES // KR, bin_loop, 0)

    for f in range(6):
        for copy in mig_copies(f, f):
            copy.wait_recv()

    def arrival_prep(f, carry):
        for b in range(FACE // 8):
            live = (sub8 + 8 * b) < arr_rows[f]
            prep(
                pl.multiple_of(RES + f * FACE + 8 * b, 8),
                [arr_pos[d, f, 8 * b : 8 * b + 8, :] for d in range(3)],
                [arr_vel[d, f, 8 * b : 8 * b + 8, :] for d in range(3)],
                jnp.where(live, 1.0, 0.0),
            )
        return carry

    lax.fori_loop(0, 6, arrival_prep, 0)
    for d in range(3):
        for h in range(2):
            half = slice(128 * h, 128 * h + 128)
            bpack[d, h : h + 1, :] = start[d][:, half]
            bpack[3 + d, h : h + 1, :] = bead_vel[d][:, half]
    lane8 = lax.broadcasted_iota(jnp.int32, (8, 128), 1) + 128 * sub8
    bead_here = (lane8 < CHAIN * chains[0]) & (sub8 < 2)
    prep(
        SOLV,
        [bpack[d] for d in range(3)],
        [bpack[3 + d] for d in range(3)],
        jnp.where(bead_here, bead_mass, 0.0),
    )
    lax.fori_loop(RES // KR, SOLV // KR, bin_loop, 0)
    bin_rows(SOLV, 2)

    for c in range(4):
        for h in range(2):
            value = acc[pl.ds(h * TROWS + c, LEVELS, stride=8), :]
            if c > 0:
                value += acc[pl.ds(h * TROWS + c + 3, LEVELS, stride=8), :]
            mom[c, 0:LEVELS, 128 * h : 128 * h + 128] = value
    for c in range(4):
        sz[c : c + 1, :] = mom[c, 32:33, :]
        sx[2 * c : 2 * c + 2, :] = mom[c, 33:35, :]
        sy[2 * c : 2 * c + 2, :] = mom[c, 35:37, :]
        se[c : c + 1, :] = mom[c, 37:38, :]

    def halo_copies(src, dst, ss, rs, sign):
        copies = []
        for i, (dx, dy, dz) in enumerate(HALO):
            s = src[min(i, 3)]
            t = dst[i] if i < 3 else dst[3].at[i - 3]
            copies.append(
                pltpu.make_async_remote_copy(
                    src_ref=s,
                    dst_ref=t,
                    send_sem=ss.at[i],
                    recv_sem=rs.at[i],
                    device_id=device(sign * dx, sign * dy, dz),
                    device_id_type=MESH,
                )
            )
        return copies

    halo = halo_copies((sx, sy, sz, se), (rx, ry, rz, re), halo_ss, halo_rs, 1)
    for copy in halo:
        copy.start()

    row_c = lax.broadcasted_iota(jnp.int32, (1, 128), 1)
    block = row_c // 4
    comp = row_c % 4
    bx = block // 6 - 1
    by = (block // 2) % 3 - 1
    wrap_x = jnp.where(ix + bx < 0, -128.0, jnp.where(ix + bx > 7, 128.0, 0.0))
    wrap_y = jnp.where(iy + by < 0, -128.0, jnp.where(iy + by > 7, 128.0, 0.0))
    image = jnp.where(comp == 0, wrap_x, jnp.where(comp == 1, wrap_y, 0.0))
    wrapped = (comp == 2) & (block % 2 == 1)
    centre = anchor[2] + 16.0
    G_s[...] = jnp.zeros_like(G_s)

    def forces(exchange):
        own = slot(0, 0, 0)
        for k in range(18):
            if k == own:
                G_s[4 * k : 4 * k + 4, :] = psend[exchange]
            else:
                G_s[4 * k : 4 * k + 4, :] = ghost[exchange, k]
        GT = G_s[...].T + image
        turns = jnp.floor((GT - centre) * (1.0 / 64.0) + 0.5)
        GT_s[...] = jnp.where(wrapped, GT - 64.0 * turns, GT)
        here = [
            [
                jnp.broadcast_to(psend[exchange, d : d + 1, 128 * h : 128 * h + 128], (8, 128))
                for d in range(3)
            ]
            for h in range(2)
        ]

        def group(j, sums):
            tile = GT_s[pl.ds(pl.multiple_of(8 * j, 8), 8), :]
            sums = list(sums)
            for k in range(18):
                other = [
                    jnp.broadcast_to(tile[:, 4 * k + d : 4 * k + d + 1], (8, 128))
                    for d in range(3)
                ]
                for h in range(2):
                    differ = [here[h][d] - other[d] for d in range(3)]
                    square = (
                        differ[0] * differ[0] + differ[1] * differ[1] + differ[2] * differ[2]
                    )
                    inside = (square < cut_square) & (square > 0.25)
                    inverse = 1.0 / jnp.where(inside, square, 1.0)
                    sixth = inverse * inverse * inverse
                    weight = jnp.where(inside, (48.0 * sixth - 24.0) * sixth * inverse, 0.0)
                    for d in range(3):
                        sums[3 * h + d] = sums[3 * h + d] + weight * differ[d]
            return tuple(sums)

        zero = jnp.zeros((8, 128), F32)
        sums = lax.fori_loop(0, 32, group, (zero,) * 6)
        for h in range(2):
            for d in range(3):
                F_s[d : d + 1, 128 * h : 128 * h + 128] = jnp.sum(
                    sums[3 * h + d], axis=0, keepdims=True
                )
        pieces = split3(jnp.concatenate([psend[exchange], psend[exchange]], 0))
        hot = D_s[...]
        differ = nn(pieces[0], hot) + nn(pieces[1], hot) + nn(pieces[2], hot)
        square = jnp.sum(jnp.where(sub256 < 3, differ * differ, 0.0), axis=0, keepdims=True)
        weight = jnp.where(bond_live, -spring / (1.0 - square / reach_square), 0.0)
        pieces = split3(weight * differ)
        pull = nt(pieces[0], hot) + nt(pieces[1], hot) + nt(pieces[2], hot)
        return [F_s[d : d + 1, :] + pull[d : d + 1, :] for d in range(3)]

    sub256 = lax.broadcasted_iota(jnp.int32, (8, 256), 0)
    F_s[...] = jnp.zeros_like(F_s)
    bead_arrive(0)
    push = forces(0)

    for copy in halo_copies((sx, sy, sz, se), (rx, ry, rz, re), halo_ss, halo_rs, -1):
        copy.wait_recv()
    zero_face = jnp.zeros((32, 256), F32)
    spread = []
    for c in range(4):
        edge = jnp.where(
            lane256 < 16,
            re[0, c : c + 1, :],
            jnp.where(
                lane256 < 32,
                re[1, c : c + 1, :],
                jnp.where(lane256 < 64, re[2, c : c + 1, :], re[3, c : c + 1, :]),
            ),
        )
        low_half = row32 < 16
        vx = jnp.where(low_half, rx[2 * c : 2 * c + 1, :], rx[2 * c + 1 : 2 * c + 2, :])
        vy = jnp.where(low_half, ry[2 * c : 2 * c + 1, :], ry[2 * c + 1 : 2 * c + 2, :])
        spread.append(
            jnp.concatenate(
                [
                    jnp.where(mask_face, vx, zero_face),
                    jnp.where(mask_face, vy, zero_face),
                    jnp.where(mask_edge, edge, zero_face),
                ],
                1,
            )
        )
    pieces = split3(jnp.concatenate(spread, 0))
    moved = nn(pieces[0], E_s[...]) + nn(pieces[1], E_s[...]) + nn(pieces[2], E_s[...])
    total = []
    for c in range(4):
        value = mom[c, 0:32, :] + moved[32 * c : 32 * c + 32, :]
        total.append(value + jnp.where(row32 == 0, rz[c : c + 1, :], 0.0))
    scale = 1.0 / jnp.maximum(total[0], 1.0)
    eye = (
        lax.broadcasted_iota(jnp.int32, (32, 32), 0) == lax.broadcasted_iota(jnp.int32, (32, 32), 1)
    )
    axis_here = nt(as_bf(eye), cell_axis[...].astype(F32).astype(BF))
    parts = [None] * 8
    for d in range(3):
        parts[d], parts[3 + d] = split2(total[1 + d] * scale)
    parts[6] = axis_here
    parts[7] = zero_face
    for c in range(8):
        for h in range(2):
            T_f[pl.ds(h * TROWS + c, 32, stride=8), :] = parts[c][:, 128 * h : 128 * h + 128]
    picked = nt(jnp.concatenate(parts[:7], 0).astype(BF), E_s[...])
    for q in range(4):
        if q < 3:
            value = picked[32 * q : 32 * q + 32, :] + picked[96 + 32 * q : 128 + 32 * q, :]
            uz[q : q + 1, :] = parts[q][0:1, :] + parts[3 + q][0:1, :]
        else:
            value = picked[192:224, :]
            uz[q : q + 1, :] = parts[6][0:1, :]
        vx = jnp.where(mask_face, value[:, 0:256], 0.0)
        vy = jnp.where(mask_face, value[:, 256:512], 0.0)
        ve = jnp.where(mask_edge, value[:, 512:768], 0.0)
        for j in range(2):
            half = slice(16 * j, 16 * j + 16)
            ux[2 * q + j : 2 * q + j + 1, :] = jnp.sum(vx[half], axis=0, keepdims=True)
            uy[2 * q + j : 2 * q + j + 1, :] = jnp.sum(vy[half], axis=0, keepdims=True)
        ue[q : q + 1, :] = jnp.sum(ve, axis=0, keepdims=True)
    info = halo_copies((ux, uy, uz, ue), (gx_, gy_, gz_, ge), info_ss, info_rs, -1)
    for copy in info:
        copy.start()
    for copy in halo_copies((ux, uy, uz, ue), (gx_, gy_, gz_, ge), info_ss, info_rs, 1):
        copy.wait_recv()

    def halo_level(level, channel, value):
        for h in range(2):
            row = h * TROWS + 8 * level + channel
            T_f[row : row + 1, :] = value[:, 128 * h : 128 * h + 128]

    for q in range(4):
        edge = jnp.where(
            lane256 < 16,
            ge[0, q : q + 1, :],
            jnp.where(
                lane256 < 32,
                ge[1, q : q + 1, :],
                jnp.where(lane256 < 64, ge[2, q : q + 1, :], ge[3, q : q + 1, :]),
            ),
        )
        edge = jnp.where(lane256 < 65, edge, 0.0)
        values = [gz_[q : q + 1, :]]
        values += [gx_[2 * q + j : 2 * q + j + 1, :] for j in range(2)]
        values += [gy_[2 * q + j : 2 * q + j + 1, :] for j in range(2)]
        values += [edge]
        for i, value in enumerate(values):
            if q < 3:
                high, low = split2(value)
                halo_level(32 + i, q, high)
                halo_level(32 + i, 3 + q, low)
            else:
                halo_level(32 + i, 6, value)
                halo_level(32 + i, 7, jnp.zeros((1, 256), F32))
    for h in range(2):
        half = slice(128 * h, 128 * h + 128)
        T_s[:, half] = T_f[h * TROWS : h * TROWS + TROWS, :].astype(BF)

    def look_rows(row0, count):
        hot = jnp.concatenate([hot_lo(row0 + r) for r in range(count)], 1)
        found = nn(T_s[...], hot)
        for r in range(count):
            row = row0 + r
            level = rows_of(hi_s, row, 8).astype(jnp.int32)
            values = [
                found[8 * j : 8 * j + 8, 128 * r : 128 * r + 128] for j in range(LEVELS)
            ]
            bit = 1
            while len(values) > 1:
                odd = (level & bit) != 0
                values = [
                    jnp.where(odd, values[i + 1], values[i]) if i + 1 < len(values) else values[i]
                    for i in range(0, len(values), 2)
                ]
                bit = 2 * bit
            V_s[pl.ds(pl.multiple_of(row * 8, 8), 8), :] = values[0]

    def collide(row0, v):
        read = [V_s[pl.ds(row0 * 8 + c, 8, stride=8), :] for c in range(7)]
        u = [read[d] + read[3 + d] for d in range(3)]
        index = read[6].astype(jnp.int32)
        n = [
            jnp.take_along_axis(axis_tab[8 * d : 8 * d + 8, :], index, axis=1) for d in range(3)
        ]
        return rotated(v, u, n)

    def emit(row0, p, v, live):
        new = collide(row0, v)
        for d in range(3):
            offset = p[d] - jnp.floor(p[d]) - 0.5
            vel_out[d, pl.ds(row0, 8), :] = jnp.where(live, new[d], 0.0)
            pos_out[d, pl.ds(row0, 8), :] = jnp.where(
                live, offset + 3.0 * step_size * new[d], 0.0
            )

    def look_resident(b, carry):
        look_rows(b * KR, KR)
        for i in range(KR // 8):
            r = pl.multiple_of(b * KR + 8 * i, 8)
            emit(
                r,
                [sol_pos[d, pl.ds(r, 8), :] for d in range(3)],
                [sol_vel[d, pl.ds(r, 8), :] for d in range(3)],
                sub8 + r < sol_rows[0],
            )
        return carry

    def look_arrival(f, carry):
        look_rows(RES + f * FACE, FACE)
        for i in range(FACE // 8):
            emit(
                pl.multiple_of(RES + f * FACE + 8 * i, 8),
                [arr_pos[d, f, 8 * i : 8 * i + 8, :] for d in range(3)],
                [arr_vel[d, f, 8 * i : 8 * i + 8, :] for d in range(3)],
                (sub8 + 8 * i) < arr_rows[f],
            )
        return carry

    look_rows(SOLV, 2)
    new = collide(SOLV, [bpack[3 + d] for d in range(3)])
    speed = []
    for d in range(3):
        W_s[d] = new[d]
        speed.append(jnp.concatenate([W_s[d, 0:1, :], W_s[d, 1:2, :]], 1))

    half_kick = 0.5 * step_size / bead_mass
    gone = [jnp.zeros((1, 256), F32)] * 3
    for substep in range(3):
        speed = [speed[d] + half_kick * push[d] for d in range(3)]
        gone = [gone[d] + step_size * speed[d] for d in range(3)]
        place(substep + 1, [start[d] + gone[d] for d in range(3)])
        bead_send(substep + 1)
        if substep == 0:
            lax.fori_loop(0, 6, look_arrival, 0)
        else:
            lax.fori_loop(8 * (substep - 1), 8 * substep, look_resident, 0)
        bead_arrive(substep + 1)
        push = forces(substep + 1)
        speed = [speed[d] + half_kick * push[d] for d in range(3)]
    for d in range(3):
        bpos_out[d] = jnp.where(bead_live, gone[d], 0.0)
        bvel_out[d] = jnp.where(bead_live, speed[d], 0.0)

    for g in range(6):
        for copy in mig_copies(g, g ^ 1):
            copy.wait_send()
    for copy in halo:
        copy.wait_send()
    for copy in info:
        copy.wait_send()
    for exchange in range(4):
        for dx, dy, dz in OFFSETS:
            bead_copy(exchange, (dx, dy, dz), slot(-dx, -dy, dz)).wait_send()


def shards(
    sol_pos,
    sol_vel,
    sol_rows,
    mig_pos,
    mig_vel,
    mig_rows,
    bead_pos,
    bead_vel,
    bead_chains,
    bond_list,
    cell_axis,
    shift,
):
    vmem = pl.BlockSpec(memory_space=pltpu.VMEM)
    smem = pl.BlockSpec(memory_space=pltpu.SMEM)
    bonds = jnp.pad(bond_list.reshape(2, 1, BONDS), ((0, 0), (0, 0), (0, 256 - BONDS)))
    dma = pltpu.SemaphoreType.DMA
    f32 = lambda *shape: pltpu.VMEM(shape, F32)
    bf = lambda *shape: pltpu.VMEM(shape, BF)
    outs = pl.pallas_call(
        kernel,
        out_shape=(
            jax.ShapeDtypeStruct((3, SOLV, 128), F32),
            jax.ShapeDtypeStruct((3, SOLV, 128), F32),
            jax.ShapeDtypeStruct((3, 1, BEADS), F32),
            jax.ShapeDtypeStruct((3, 1, BEADS), F32),
        ),
        in_specs=[smem] * 4 + [vmem] * 9,
        out_specs=(vmem,) * 4,
        scratch_shapes=[
            f32(ALL, 128),
            f32(ALL, 128),
            f32(ALL * 8, 128),
            f32(2 * TROWS, 128),
            bf(256, 128),
            bf(TROWS, 128),
            f32(3, 6, FACE, 128),
            f32(3, 6, FACE, 128),
            pltpu.VMEM((6, 1, 128), jnp.int32),
            pltpu.VMEM((6, 1, 128), jnp.int32),
            f32(6, 8, 128),
            f32(4, 40, 256),
            bf(768, 256),
            bf(256, 256),
            f32(8, 256),
            f32(8, 256),
            f32(4, 256),
            f32(4, 256),
            f32(8, 256),
            f32(8, 256),
            f32(4, 256),
            f32(4, 4, 256),
            f32(8, 256),
            f32(8, 256),
            f32(4, 256),
            f32(4, 256),
            f32(8, 256),
            f32(8, 256),
            f32(4, 256),
            f32(4, 4, 256),
            f32(4, 32, 256),
            f32(2 * TROWS, 128),
            bf(TROWS, 256),
            f32(4, 4, 256),
            f32(4, 18, 4, 256),
            f32(128, 256),
            f32(256, 128),
            f32(8, 256),
            f32(3, 8, 128),
            dma((3, 6)),
            dma((3, 6)),
            dma((7,)),
            dma((7,)),
            dma((7,)),
            dma((7,)),
            dma((4, 18)),
            dma((4, 18)),
        ],
        compiler_params=pltpu.CompilerParams(
            collective_id=0, has_side_effects=True, vmem_limit_bytes=60 * 1024 * 1024
        ),
        name="interval",
    )(
        sol_rows.reshape(1),
        mig_rows.reshape(6),
        bead_chains.reshape(1),
        shift,
        sol_pos.reshape(3, RES, 128),
        sol_vel.reshape(3, RES, 128),
        mig_pos.reshape(3, 6, FACE, 128),
        mig_vel.reshape(3, 6, FACE, 128),
        bead_pos.reshape(3, 1, BEADS),
        bead_vel.reshape(3, 1, BEADS),
        bonds,
        cell_axis.reshape(256, 32),
        jnp.asarray(axis_rows()),
    )
    pos, vel, bpos, bvel = outs
    return (
        pos.reshape(3, 1, 1, 1, SOLV * 128),
        vel.reshape(3, 1, 1, 1, SOLV * 128),
        bpos.reshape(3, 1, 1, 1, BEADS),
        bvel.reshape(3, 1, 1, 1, BEADS),
    )


def solution(mesh):
    return jax.shard_map(
        shards,
        mesh=mesh,
        in_specs=(
            P(None, "gx", "gy", "gz", None),
            P(None, "gx", "gy", "gz", None),
            P("gx", "gy", "gz"),
            P(None, "gx", "gy", "gz", None, None),
            P(None, "gx", "gy", "gz", None, None),
            P("gx", "gy", "gz", None),
            P(None, "gx", "gy", "gz", None),
            P(None, "gx", "gy", "gz", None),
            P("gx", "gy", "gz"),
            P(None, "gx", "gy", "gz", None),
            P("gx", "gy", "gz"),
            P(),
        ),
        out_specs=(
            P(None, "gx", "gy", "gz", None),
            P(None, "gx", "gy", "gz", None),
            P(None, "gx", "gy", "gz", None),
            P(None, "gx", "gy", "gz", None),
        ),
        check_vma=False,
    )
```

time: 604 us -> 90.3 us (0.15); the launches traced: 592 us -> 90 us
  local copies, waits for them, and re-layouts: 245 us -> 5.57 us
  matrix products: 128 us -> 0 us
  other arithmetic: 101 us -> 0 us
  Pallas kernels: 0 us -> 82.5 us
  starting transfers between devices: 57.5 us -> 0 us
  waiting for transfers between devices: 47.3 us -> 0 us
  loops' own time: 11 us -> 0 us
    dynamic_slice x268 -> x0, local copies, waits for them, and re-layouts: 167 us -> none  [binned_sums(): lax.scan(binned_add_block, start, (moment_blocks, plane_blocks, depth_blo...]
    dot_general x147 -> x0, matrix products: 128 us -> none  [the longest x67 62.6 us: binned_add_block(): lax.dot_general(spread, plane_hot, (((1,), (1,)), ((), ())), precision=la...]
    pallas_call x0 -> x1, Pallas kernels: none -> 82.5 us  [shards(): pl.pallas_call(kernel, out_shape=(jax.ShapeDtypeStruct((3, SOLV, 128), F3...]
    reduce_sum x284 -> x0, other arithmetic: 65.3 us -> none  [the longest x108 33.8 us: pair_add_block(): return (running + jnp.sum(weight[None] * differ, axis=2), None)]
    ppermute x36 -> x0, starting transfers between devices: 57.4 us -> none  [the longest x12 30.6 us: with_halo_2(): after = lax.ppermute(first, axis, down)]
    ppermute x36 -> x0, waiting for transfers between devices: 47.3 us -> none  [the longest x6 24 us: shifted(): lax.ppermute(value, axis, [(i, (i + by) % peers) for i in range(peers)])]
    dynamic_update_slice x67 -> x0, local copies, waits for them, and re-layouts: 41.5 us -> none  [binned_lookup(): picked = lax.map(read_block, (plane_blocks, depth_blocks))]
    reshape x77 -> x0, local copies, waits for them, and re-layouts: 15.2 us -> none  [the longest x67 7.05 us: read_block(): jnp.dot(table, plane_hot, precision=lax.Precision.HIGHEST)]
  transfers between devices with their start and end apart: 36 -> 0, of which waited for: 17 -> 0; matrix products, arithmetic and copies ran while one was open for 40% -> 0% of each run, Pallas kernels for 0% -> 0%
where the time goes in v1:
time: 90.3 us; the launch traced here: 90 us
  Pallas kernels  82.5 us (91%)
  local copies, waits for them, and re-layouts  5.57 us (6%)
  between operations  1.95 us (2%)
    pallas_call x1, Pallas kernels, shards(): pl.pallas_call(kernel, out_shape=(jax.ShapeDtypeStruct((3, SOLV, 128), F3...  82.5 us
    unnamed x12, local copies, waits for them, and re-layouts  4.98 us

profile of v1, /device:TPU:0, one launch (start us, length us, event | category | flops | bytes accessed | tf_op | source)
XLA Modules:
  0.0 90.0 jit_solution(7701943972754221404)
XLA Ops:
  1.9 0.0 copy-start.3
  1.9 0.7 copy-done.3
  2.6 0.6 pad.4.bond_list
  3.2 82.5 %interval.1 = (f32[3,528,128]{2,1,0:T(8,128)}, f32[3,528,128]{2,1,0:T(8,128)}, f32[3,1,256]{2,1,0:T(1,128)}, f32[3,1,256]{2,1,0:T(1,128)}) custom-call(s32[1]{0:T(128)} %bitcast.19.sol_rows, s32[6]{0:T(128)} %bitcast.33, s32[1]{0:T(128)} %bitcast.20.chains, s32[3]{0:T(128)} %shift.1, f32[3,384,128]{2,1,0:T(8,128)} %bitcast.23, f32[3,384,128]{2,1,0:T(8,128)} %bitcast.24, ...), custom_call_target="tpu_custom_call" | custom-call | tf_op jit(solution)/shard_map/interval/pallas_call | solution.py:717
  85.7 0.0 copy-start
  85.7 2.2 %copy.31 = f32[3,1,1,1,67584]{4,3,2,1,0:T(1,128)} copy(f32[3,1,1,1,67584]{4,3,2,1,0:T(1,128)} %bitcast.22) | data formatting | bytes 1622016
  87.9 0.0 copy-done
  87.9 0.0 copy-start.2
  87.9 0.9 copy.32
  88.8 0.0 copy-done.2
  88.8 0.0 copy-start.1
  88.8 0.6 copy.33
  89.3 0.1 copy-done.1
  89.4 0.6 copy.34
Async XLA Ops:
  1.9 0.7 copy-start.3
  85.7 2.2 %copy-start = (f32[3,528,128]{2,1,0:T(8,128)S(1)}, f32[3,528,128]{2,1,0:T(8,128)}, u32[]{:S(2)}) copy-start(f32[3,528,128]{2,1,0:T(8,128)} %get-tuple-element.9) | copy-start | bytes 2433028
  87.9 0.9 copy-start.2
  88.8 0.7 copy-start.1

commit v2 on v1

--- a/solution.py
+++ b/solution.py
@@ -102,8 +102,8 @@
     mig_rows,
     chains,
     shift,
-    sol_pos,
-    sol_vel,
+    sol_pos_hbm,
+    sol_vel_hbm,
     mig_pos,
     mig_vel,
     bead_pos,
@@ -111,10 +111,15 @@
     bond_list,
     cell_axis,
     axis_tab,
-    pos_out,
-    vel_out,
+    off_hbm,
+    vel_hbm,
     bpos_out,
     bvel_out,
+    sol_pos,
+    sol_vel,
+    off_out,
+    vel_out,
+    bond_s,
     lo_s,
     hi_s,
     V_s,
@@ -152,7 +157,9 @@
     ghost,
     G_s,
     GT_s,
-    F_s,
+    P_s,
+    M_s,
+    A_s,
     W_s,
     mig_ss,
     mig_rs,
@@ -162,6 +169,8 @@
     info_rs,
     bead_ss,
     bead_rs,
+    in_sem,
+    out_sem,
 ):
     ix = lax.axis_index("gx")
     iy = lax.axis_index("gy")
@@ -177,6 +186,23 @@
     barrier = pltpu.get_barrier_semaphore()
     for off in OFFSETS:
         pl.semaphore_signal(barrier, inc=1, device_id=device(*off), device_id_type=MESH)
+
+    HALF = RES // 2
+
+    def in_copies(chunk):
+        part = pl.ds(chunk * HALF, HALF)
+        return [
+            pltpu.make_async_copy(
+                sol_pos_hbm.at[:, part], sol_pos.at[:, part], in_sem.at[0, chunk]
+            ),
+            pltpu.make_async_copy(
+                sol_vel_hbm.at[:, part], sol_vel.at[:, part], in_sem.at[1, chunk]
+            ),
+        ]
+
+    for chunk in range(2):
+        for copy in in_copies(chunk):
+            copy.start()
 
     iota_lo[...] = lax.broadcasted_iota(jnp.int32, (256, 128), 0).astype(F32).astype(BF)
     iota_hi[...] = (
@@ -243,34 +269,6 @@
         )
         return carry
 
-    lax.fori_loop(0, RES // 8, resident_prep, 0)
-
-    row32 = lax.broadcasted_iota(jnp.int32, (32, 256), 0)
-    col32 = lax.broadcasted_iota(jnp.int32, (32, 256), 1)
-    mask_face = (col32 % 16) == (row32 % 16)
-    mask_edge = (
-        ((col32 < 32) & (row32 == 0))
-        | ((col32 >= 32) & (col32 < 64) & (col32 - 32 == row32))
-        | ((col32 == 64) & (row32 == 0))
-    )
-    er = lax.broadcasted_iota(jnp.int32, (256, 256), 0)
-    ec = lax.broadcasted_iota(jnp.int32, (256, 256), 1)
-
-    def as_bf(mask):
-        return jnp.where(mask, 1.0, 0.0).astype(BF)
-
-    E_s[0:256, :] = as_bf(ec == er // 16)
-    E_s[256:512, :] = as_bf(ec == (er // 16) * 16)
-    target = jnp.where(er < 16, er, jnp.where(er < 32, (er - 16) * 16, 0))
-    E_s[512:768, :] = as_bf(ec == target)
-    first = jnp.where(bond_live, bond_list[0], -1)
-    second = jnp.where(bond_live, bond_list[1], -1)
-    D_s[...] = (
-        jnp.where(er == first, 1.0, 0.0) - jnp.where(er == second, 1.0, 0.0)
-    ).astype(BF)
-
-    pl.semaphore_wait(barrier, len(OFFSETS))
-
     faces = [(-1, 0, 0), (1, 0, 0), (0, -1, 0), (0, 1, 0), (0, 0, 1), (0, 0, 1)]
 
     def mig_copies(g, f):
@@ -317,11 +315,6 @@
         for off in OFFSETS:
             bead_copy(exchange, off, slot(*off)).wait_recv()
 
-    bead_send(0)
-    for g in range(6):
-        for copy in mig_copies(g, g ^ 1):
-            copy.start()
-
     def hot_lo(row):
         lo_b = rows_of(lo_s, row, 16).astype(BF)
         return jnp.concatenate(
@@ -358,7 +351,21 @@
         bin_rows(b * KR, KR)
         return carry
 
-    lax.fori_loop(0, RES // KR, bin_loop, 0)
+    for copy in in_copies(0):
+        copy.wait()
+    lax.fori_loop(0, HALF // 8, resident_prep, 0)
+    lax.fori_loop(0, HALF // KR, bin_loop, 0)
+    for copy in in_copies(1):
+        copy.wait()
+    lax.fori_loop(HALF // 8, RES // 8, resident_prep, 0)
+
+    pl.semaphore_wait(barrier, len(OFFSETS))
+    bead_send(0)
+    for g in range(6):
+        for copy in mig_copies(g, g ^ 1):
+            copy.start()
+
+    lax.fori_loop(HALF // KR, RES // KR, bin_loop, 0)
 
     for f in range(6):
         for copy in mig_copies(f, f):
@@ -425,7 +432,32 @@
     for copy in halo:
         copy.start()
 
-    row_c = lax.broadcasted_iota(jnp.int32, (1, 128), 1)
+    row32 = lax.broadcasted_iota(jnp.int32, (32, 256), 0)
+    col32 = lax.broadcasted_iota(jnp.int32, (32, 256), 1)
+    mask_face = (col32 % 16) == (row32 % 16)
+    mask_edge = (
+        ((col32 < 32) & (row32 == 0))
+        | ((col32 >= 32) & (col32 < 64) & (col32 - 32 == row32))
+        | ((col32 == 64) & (row32 == 0))
+    )
+    er = lax.broadcasted_iota(jnp.int32, (256, 256), 0)
+    ec = lax.broadcasted_iota(jnp.int32, (256, 256), 1)
+
+    def as_bf(mask):
+        return jnp.where(mask, 1.0, 0.0).astype(BF)
+
+    E_s[0:256, :] = as_bf(ec == er // 16)
+    E_s[256:512, :] = as_bf(ec == (er // 16) * 16)
+    target = jnp.where(er < 16, er, jnp.where(er < 32, (er - 16) * 16, 0))
+    E_s[512:768, :] = as_bf(ec == target)
+    bond_s[:, :, 0:BONDS] = bond_list[...]
+    first = jnp.where(bond_live, bond_s[0], -1)
+    second = jnp.where(bond_live, bond_s[1], -1)
+    D_s[...] = (
+        jnp.where(er == first, 1.0, 0.0) - jnp.where(er == second, 1.0, 0.0)
+    ).astype(BF)
+
+    row_c = lax.broadcasted_iota(jnp.int32, (72, 256), 0)
     block = row_c // 4
     comp = row_c % 4
     bx = block // 6 - 1
@@ -435,54 +467,82 @@
     image = jnp.where(comp == 0, wrap_x, jnp.where(comp == 1, wrap_y, 0.0))
     wrapped = (comp == 2) & (block % 2 == 1)
     centre = anchor[2] + 16.0
+    upper = ((comp == 0) & (bx == 1)) | ((comp == 1) & (by == 1))
     G_s[...] = jnp.zeros_like(G_s)
 
     def forces(exchange):
         own = slot(0, 0, 0)
         for k in range(18):
             if k == own:
-                G_s[4 * k : 4 * k + 4, :] = psend[exchange]
+                G_s[0:4, :] = psend[exchange]
+                P_s[4 * k : 4 * k + 4, :] = psend[exchange]
             else:
-                G_s[4 * k : 4 * k + 4, :] = ghost[exchange, k]
-        GT = G_s[...].T + image
-        turns = jnp.floor((GT - centre) * (1.0 / 64.0) + 0.5)
-        GT_s[...] = jnp.where(wrapped, GT - 64.0 * turns, GT)
-        here = [
-            [
-                jnp.broadcast_to(psend[exchange, d : d + 1, 128 * h : 128 * h + 128], (8, 128))
-                for d in range(3)
-            ]
-            for h in range(2)
-        ]
-
-        def group(j, sums):
-            tile = GT_s[pl.ds(pl.multiple_of(8 * j, 8), 8), :]
-            sums = list(sums)
-            for k in range(18):
-                other = [
-                    jnp.broadcast_to(tile[:, 4 * k + d : 4 * k + d + 1], (8, 128))
-                    for d in range(3)
-                ]
-                for h in range(2):
-                    differ = [here[h][d] - other[d] for d in range(3)]
-                    square = (
-                        differ[0] * differ[0] + differ[1] * differ[1] + differ[2] * differ[2]
-                    )
-                    inside = (square < cut_square) & (square > 0.25)
-                    inverse = 1.0 / jnp.where(inside, square, 1.0)
-                    sixth = inverse * inverse * inverse
-                    weight = jnp.where(inside, (48.0 * sixth - 24.0) * sixth * inverse, 0.0)
-                    for d in range(3):
-                        sums[3 * h + d] = sums[3 * h + d] + weight * differ[d]
-            return tuple(sums)
-
-        zero = jnp.zeros((8, 128), F32)
-        sums = lax.fori_loop(0, 32, group, (zero,) * 6)
-        for h in range(2):
-            for d in range(3):
-                F_s[d : d + 1, 128 * h : 128 * h + 128] = jnp.sum(
-                    sums[3 * h + d], axis=0, keepdims=True
-                )
+                P_s[4 * k : 4 * k + 4, :] = ghost[exchange, k]
+        GT_s[...] = G_s[...].T
+        at = P_s[...] + image
+        turns = jnp.floor((at - centre) * (1.0 / 64.0) + 0.5)
+        at = jnp.where(wrapped, at - 64.0 * turns, at)
+        at = jnp.where(upper & (at < -500.0), -3.0 * far_point, at)
+        P_s[...] = at
+        M_s[0:24, :] = 0.5 * (at[0:24] + at[48:72])
+        M_s[24:32, :] = 0.5 * (at[24:32] + at[40:48])
+
+        def group(j, carry):
+            here = []
+            for t in range(2):
+                tile = GT_s[pl.ds(pl.multiple_of(16 * j + 8 * t, 8), 8), :]
+                here.append([jnp.broadcast_to(tile[:, d : d + 1], (8, 128)) for d in range(3)])
+            twice = [here[t][1] + here[t][1] for t in range(2)]
+            sums = [jnp.zeros((8, 128), F32) for i in range(6)]
+
+            def choose(mask, a, b):
+                return [jnp.where(mask, a[d], b[d]) for d in range(3)]
+
+            def add(t, other):
+                differ = [here[t][d] - other[d] for d in range(3)]
+                square = differ[0] * differ[0] + differ[1] * differ[1] + differ[2] * differ[2]
+                inverse = 1.0 / jnp.where(square > 0.25, square, 1.0e6)
+                sixth = inverse * inverse * inverse
+                weight = jnp.maximum(48.0 * sixth - 24.0, 0.0) * sixth * inverse
+                for d in range(3):
+                    sums[3 * t + d] = sums[3 * t + d] + weight * differ[d]
+
+            for h in range(2):
+                half = slice(128 * h, 128 * h + 128)
+
+                def row(ref, r):
+                    return jnp.broadcast_to(ref[r : r + 1, half], (8, 128))
+
+                def ghost_at(dx, dy, dz):
+                    return [row(P_s, 4 * slot(dx, dy, dz) + d) for d in range(3)]
+
+                for dz in (0, 1):
+                    inner = ghost_at(0, 0, dz)
+                    for t in range(2):
+                        add(t, inner)
+                    low, high = ghost_at(0, -1, dz), ghost_at(0, 1, dz)
+                    half_way = row(M_s, 4 * slot(0, -1, dz) + 1)
+                    for t in range(2):
+                        add(t, choose(here[t][1] < half_way, low, high))
+                    near = [[], []]
+                    for dy in (0, -1, 1):
+                        low, high = ghost_at(-1, dy, dz), ghost_at(1, dy, dz)
+                        half_way = row(M_s, 4 * slot(-1, dy, dz))
+                        for t in range(2):
+                            near[t].append(choose(here[t][0] < half_way, low, high))
+                    for t in range(2):
+                        side, low, high = near[t]
+                        add(t, side)
+                        add(t, choose(twice[t] < low[1] + high[1], low, high))
+            for t in range(2):
+                for d in range(3):
+                    A_s[pl.ds(pl.multiple_of(256 * d + 16 * j + 8 * t, 8), 8), :] = sums[3 * t + d]
+            return carry
+
+        lax.fori_loop(0, 16, group, 0)
+        ones = jnp.ones((8, 128), BF)
+        pieces = split3(A_s[...])
+        pair = nt(ones, pieces[0]) + nt(ones, pieces[1]) + nt(ones, pieces[2])
         pieces = split3(jnp.concatenate([psend[exchange], psend[exchange]], 0))
         hot = D_s[...]
         differ = nn(pieces[0], hot) + nn(pieces[1], hot) + nn(pieces[2], hot)
@@ -490,10 +550,9 @@
         weight = jnp.where(bond_live, -spring / (1.0 - square / reach_square), 0.0)
         pieces = split3(weight * differ)
         pull = nt(pieces[0], hot) + nt(pieces[1], hot) + nt(pieces[2], hot)
-        return [F_s[d : d + 1, :] + pull[d : d + 1, :] for d in range(3)]
+        return [pair[0:1, 256 * d : 256 * d + 256] + pull[d : d + 1, :] for d in range(3)]
 
     sub256 = lax.broadcasted_iota(jnp.int32, (8, 256), 0)
-    F_s[...] = jnp.zeros_like(F_s)
     bead_arrive(0)
     push = forces(0)
 
@@ -629,10 +688,8 @@
         new = collide(row0, v)
         for d in range(3):
             offset = p[d] - jnp.floor(p[d]) - 0.5
-            vel_out[d, pl.ds(row0, 8), :] = jnp.where(live, new[d], 0.0)
-            pos_out[d, pl.ds(row0, 8), :] = jnp.where(
-                live, offset + 3.0 * step_size * new[d], 0.0
-            )
+            vel_out[d, pl.ds(row0, 8), :] = new[d]
+            off_out[d, pl.ds(row0, 8), :] = jnp.where(live, offset, 2.0)
 
     def look_resident(b, carry):
         look_rows(b * KR, KR)
@@ -664,6 +721,17 @@
         W_s[d] = new[d]
         speed.append(jnp.concatenate([W_s[d, 0:1, :], W_s[d, 1:2, :]], 1))
 
+    def out_copies(substep):
+        part = pl.ds(RES, SOLV - RES) if substep == 0 else pl.ds((substep - 1) * HALF, HALF)
+        return [
+            pltpu.make_async_copy(
+                off_out.at[:, part], off_hbm.at[:, part], out_sem.at[0, substep]
+            ),
+            pltpu.make_async_copy(
+                vel_out.at[:, part], vel_hbm.at[:, part], out_sem.at[1, substep]
+            ),
+        ]
+
     half_kick = 0.5 * step_size / bead_mass
     gone = [jnp.zeros((1, 256), F32)] * 3
     for substep in range(3):
@@ -675,12 +743,17 @@
             lax.fori_loop(0, 6, look_arrival, 0)
         else:
             lax.fori_loop(8 * (substep - 1), 8 * substep, look_resident, 0)
+        for copy in out_copies(substep):
+            copy.start()
         bead_arrive(substep + 1)
         push = forces(substep + 1)
         speed = [speed[d] + half_kick * push[d] for d in range(3)]
     for d in range(3):
-        bpos_out[d] = jnp.where(bead_live, gone[d], 0.0)
-        bvel_out[d] = jnp.where(bead_live, speed[d], 0.0)
+        bpos_out[d] = gone[d]
+        bvel_out[d] = speed[d]
+    for substep in range(3):
+        for copy in out_copies(substep):
+            copy.wait()
 
     for g in range(6):
         for copy in mig_copies(g, g ^ 1):
@@ -710,7 +783,7 @@
 ):
     vmem = pl.BlockSpec(memory_space=pltpu.VMEM)
     smem = pl.BlockSpec(memory_space=pltpu.SMEM)
-    bonds = jnp.pad(bond_list.reshape(2, 1, BONDS), ((0, 0), (0, 0), (0, 256 - BONDS)))
+    anywhere = pl.BlockSpec(memory_space=pl.ANY)
     dma = pltpu.SemaphoreType.DMA
     f32 = lambda *shape: pltpu.VMEM(shape, F32)
     bf = lambda *shape: pltpu.VMEM(shape, BF)
@@ -722,9 +795,14 @@
             jax.ShapeDtypeStruct((3, 1, BEADS), F32),
             jax.ShapeDtypeStruct((3, 1, BEADS), F32),
         ),
-        in_specs=[smem] * 4 + [vmem] * 9,
-        out_specs=(vmem,) * 4,
+        in_specs=[smem] * 4 + [anywhere] * 4 + [vmem] * 5,
+        out_specs=(anywhere, anywhere, vmem, vmem),
         scratch_shapes=[
+            f32(3, RES, 128),
+            f32(3, RES, 128),
+            f32(3, SOLV, 128),
+            f32(3, SOLV, 128),
+            pltpu.VMEM((2, 1, 256), jnp.int32),
             f32(ALL, 128),
             f32(ALL, 128),
             f32(ALL * 8, 128),
@@ -762,7 +840,9 @@
             f32(4, 18, 4, 256),
             f32(128, 256),
             f32(256, 128),
-            f32(8, 256),
+            f32(72, 256),
+            f32(32, 256),
+            f32(768, 128),
             f32(3, 8, 128),
             dma((3, 6)),
             dma((3, 6)),
@@ -772,6 +852,8 @@
             dma((7,)),
             dma((4, 18)),
             dma((4, 18)),
+            dma((2, 2)),
+            dma((2, 3)),
         ],
         compiler_params=pltpu.CompilerParams(
             collective_id=0, has_side_effects=True, vmem_limit_bytes=60 * 1024 * 1024
@@ -788,16 +870,18 @@
         mig_vel.reshape(3, 6, FACE, 128),
         bead_pos.reshape(3, 1, BEADS),
         bead_vel.reshape(3, 1, BEADS),
-        bonds,
+        bond_list.reshape(2, 1, BONDS),
         cell_axis.reshape(256, 32),
         jnp.asarray(axis_rows()),
     )
-    pos, vel, bpos, bvel = outs
+    offset, vel, bpos, bvel = outs
+    live = offset < 1.0
+    bead_live = jnp.arange(BEADS, dtype=jnp.int32) < CHAIN * bead_chains.reshape(())
     return (
-        pos.reshape(3, 1, 1, 1, SOLV * 128),
-        vel.reshape(3, 1, 1, 1, SOLV * 128),
-        bpos.reshape(3, 1, 1, 1, BEADS),
-        bvel.reshape(3, 1, 1, 1, BEADS),
+        jnp.where(live, offset + 3.0 * step_size * vel, 0.0).reshape(3, 1, 1, 1, SOLV * 128),
+        jnp.where(live, vel, 0.0).reshape(3, 1, 1, 1, SOLV * 128),
+        jnp.where(bead_live, bpos, 0.0).reshape(3, 1, 1, 1, BEADS),
+        jnp.where(bead_live, bvel, 0.0).reshape(3, 1, 1, 1, BEADS),
     )
 
 

time: 90.3 us -> 76.5 us (0.85)
  Pallas kernels: 82.5 us -> 70.3 us
  local copies, waits for them, and re-layouts: 5.57 us -> 0.65 us
  other arithmetic: 0 us -> 3.29 us
    pallas_call x1, Pallas kernels: 82.5 us -> 70.3 us  [shards(): pl.pallas_call(kernel, out_shape=(jax.ShapeDtypeStruct((3, SOLV, 128), F3...]
    unnamed x12 -> x4, local copies, waits for them, and re-layouts: 4.98 us -> 0.65 us
    select_n x0 -> x1, other arithmetic: none -> 2.7 us  [shards(): jnp.where(live, vel, 0.0).reshape(3, 1, 1, 1, SOLV * 128)]
where the time goes in v2:
time: 76.5 us; the launch traced here: 76.2 us
  Pallas kernels  70.3 us (92%)
  other arithmetic  3.29 us (4%)
  between operations  1.96 us (3%)
    pallas_call x1, Pallas kernels, shards(): pl.pallas_call(kernel, out_shape=(jax.ShapeDtypeStruct((3, SOLV, 128), F3...  70.3 us
    select_n x1, other arithmetic, shards(): jnp.where(live, vel, 0.0).reshape(3, 1, 1, 1, SOLV * 128)  2.7 us

profile of v2, /device:TPU:0, one launch (start us, length us, event | category | flops | bytes accessed | tf_op | source)
XLA Modules:
  0.0 76.2 jit_solution(15098407741100725664)
XLA Ops:
  1.9 70.3 %interval.1 = (f32[3,528,128]{2,1,0:T(8,128)}, f32[3,528,128]{2,1,0:T(8,128)}, f32[3,1,256]{2,1,0:T(1,128)}, f32[3,1,256]{2,1,0:T(1,128)}) custom-call(s32[1]{0:T(128)} %bitcast.22.sol_rows, s32[6]{0:T(128)} %bitcast.34, s32[1]{0:T(128)} %bitcast.23.chains, s32[3]{0:T(128)} %shift.1, f32[3,384,128]{2,1,0:T(8,128)} %bitcast.26, f32[3,384,128]{2,1,0:T(8,128)} %bitcast.27, ...), custom_call_target="tpu_custom_call" | custom-call | tf_op jit(solution)/shard_map/interval/pallas_call | solution.py:790
  72.3 0.0 copy-start.1
  72.3 0.0 copy-start
  72.3 0.6 copy-done.1
  73.0 0.0 copy-done
  73.0 0.6 fusion.1
  73.5 2.7 %broadcast_select_fusion = (f32[3,528,128]{2,1,0:T(8,128)}, f32[3,528,128]{2,1,0:T(8,128)}) fusion(f32[3,528,128]{2,1,0:T(8,128)} %get-tuple-element.9, f32[3,528,128]{2,1,0:T(8,128)} %get-tuple-element.8), kind=kLoop, calls=%fused_computation.1 | loop fusion | flops 1013760 | bytes 3244032 | tf_op jit(solution)/shard_map/jit(_where)/select_n | solution.py:882
  (1 shorter events, 0.0 us)
Async XLA Ops:
  72.3 0.7 copy-start.1
  72.3 0.7 copy-start

commit v3 on v2

--- a/solution.py
+++ b/solution.py
@@ -33,7 +33,7 @@
 FACE = 24
 SOLV = RES + 6 * FACE
 ALL = SOLV + 8
-KR = 24
+STEP = 2 * FACE
 BEADS = 256
 BONDS = 224
 
@@ -44,6 +44,7 @@
     for dz in (0, 1)
     if (dx, dy, dz) != (0, 0, 0)
 ]
+FACES = [(-1, 0, 0), (1, 0, 0), (0, -1, 0), (0, 1, 0), (0, 0, 1)]
 HALO = [(1, 0, 0), (0, 1, 0), (0, 0, 1), (1, 0, 1), (0, 1, 1), (1, 1, 0), (1, 1, 1)]
 
 
@@ -126,8 +127,7 @@
     acc,
     iota_lo,
     iota_hi,
-    arr_pos,
-    arr_vel,
+    limit,
     arr_rows,
     row_send,
     bpack,
@@ -171,6 +171,7 @@
     bead_rs,
     in_sem,
     out_sem,
+    entered,
 ):
     ix = lax.axis_index("gx")
     iy = lax.axis_index("gy")
@@ -184,8 +185,12 @@
         )
 
     barrier = pltpu.get_barrier_semaphore()
-    for off in OFFSETS:
-        pl.semaphore_signal(barrier, inc=1, device_id=device(*off), device_id_type=MESH)
+
+    def tell(sem):
+        for off in FACES:
+            pl.semaphore_signal(sem, inc=1, device_id=device(*off), device_id_type=MESH)
+
+    tell(barrier)
 
     HALF = RES // 2
 
@@ -258,16 +263,22 @@
             V_s[pl.ds(row0 * 8 + 4 + d, 8, stride=8), :] = low
         V_s[pl.ds(row0 * 8 + 7, 8, stride=8), :] = jnp.zeros((8, 128), F32)
 
-    def resident_prep(b, carry):
-        r = pl.multiple_of(b * 8, 8)
-        weight = jnp.where(sub8 + r < sol_rows[0], 1.0, 0.0)
-        prep(
+    limit[0 : RES // 8, :] = jnp.broadcast_to(sol_rows[0], (RES // 8, 128)).astype(jnp.int32)
+
+    def solvent(b, i):
+        r = pl.multiple_of(b * STEP + 8 * i, 8)
+        live = sub8 + r < limit[pl.ds(b * (STEP // 8) + i, 1), :]
+        return (
             r,
             [sol_pos[d, pl.ds(r, 8), :] for d in range(3)],
             [sol_vel[d, pl.ds(r, 8), :] for d in range(3)],
-            weight,
+            live,
         )
-        return carry
+
+    def prep_step(b):
+        for i in range(STEP // 8):
+            r, p, v, live = solvent(b, i)
+            prep(r, p, v, jnp.where(live, 1.0, 0.0))
 
     faces = [(-1, 0, 0), (1, 0, 0), (0, -1, 0), (0, 1, 0), (0, 0, 1), (0, 0, 1)]
 
@@ -276,14 +287,14 @@
         return [
             pltpu.make_async_remote_copy(
                 src_ref=mig_pos.at[:, g],
-                dst_ref=arr_pos.at[:, f],
+                dst_ref=sol_pos.at[:, pl.ds(RES + FACE * f, FACE)],
                 send_sem=mig_ss.at[0, g],
                 recv_sem=mig_rs.at[0, f],
                 **where,
             ),
             pltpu.make_async_remote_copy(
                 src_ref=mig_vel.at[:, g],
-                dst_ref=arr_vel.at[:, f],
+                dst_ref=sol_vel.at[:, pl.ds(RES + FACE * f, FACE)],
                 send_sem=mig_ss.at[1, g],
                 recv_sem=mig_rs.at[1, f],
                 **where,
@@ -347,42 +358,6 @@
         acc[0:TROWS, :] += sums[:, 0:128]
         acc[TROWS : 2 * TROWS, :] += sums[:, 128:256]
 
-    def bin_loop(b, carry):
-        bin_rows(b * KR, KR)
-        return carry
-
-    for copy in in_copies(0):
-        copy.wait()
-    lax.fori_loop(0, HALF // 8, resident_prep, 0)
-    lax.fori_loop(0, HALF // KR, bin_loop, 0)
-    for copy in in_copies(1):
-        copy.wait()
-    lax.fori_loop(HALF // 8, RES // 8, resident_prep, 0)
-
-    pl.semaphore_wait(barrier, len(OFFSETS))
-    bead_send(0)
-    for g in range(6):
-        for copy in mig_copies(g, g ^ 1):
-            copy.start()
-
-    lax.fori_loop(HALF // KR, RES // KR, bin_loop, 0)
-
-    for f in range(6):
-        for copy in mig_copies(f, f):
-            copy.wait_recv()
-
-    def arrival_prep(f, carry):
-        for b in range(FACE // 8):
-            live = (sub8 + 8 * b) < arr_rows[f]
-            prep(
-                pl.multiple_of(RES + f * FACE + 8 * b, 8),
-                [arr_pos[d, f, 8 * b : 8 * b + 8, :] for d in range(3)],
-                [arr_vel[d, f, 8 * b : 8 * b + 8, :] for d in range(3)],
-                jnp.where(live, 1.0, 0.0),
-            )
-        return carry
-
-    lax.fori_loop(0, 6, arrival_prep, 0)
     for d in range(3):
         for h in range(2):
             half = slice(128 * h, 128 * h + 128)
@@ -396,8 +371,56 @@
         [bpack[3 + d] for d in range(3)],
         jnp.where(bead_here, bead_mass, 0.0),
     )
-    lax.fori_loop(RES // KR, SOLV // KR, bin_loop, 0)
     bin_rows(SOLV, 2)
+    RSTEPS = RES // STEP
+    HSTEPS = RSTEPS // 2
+
+    STEPS = SOLV // STEP
+    for copy in in_copies(0):
+        copy.wait()
+    prep_step(0)
+
+    def bin_loop(b, carry):
+        @pl.when(b == 2)
+        def _():
+            pl.semaphore_wait(barrier, len(FACES))
+            for g in (4, 5, 0, 1, 2, 3):
+                for copy in mig_copies(g, g ^ 1):
+                    copy.start()
+            tell(entered.at[0])
+
+        @pl.when(b == HSTEPS - 1)
+        def _():
+            for copy in in_copies(1):
+                copy.wait()
+
+        @pl.when(b == HSTEPS)
+        def _():
+            pl.semaphore_wait(entered.at[0], len(FACES))
+            tell(entered.at[1])
+
+        @pl.when(b == HSTEPS + 2)
+        def _():
+            pl.semaphore_wait(entered.at[1], len(FACES))
+            bead_send(0)
+
+        for pair in range(3):
+
+            @pl.when(b == RSTEPS - 1 + pair)
+            def _():
+                for f in (2 * pair, 2 * pair + 1):
+                    for copy in mig_copies(f, f):
+                        copy.wait_recv()
+                    first = (RES + FACE * f) // 8
+                    limit[first : first + FACE // 8, :] = (
+                        jnp.broadcast_to(arr_rows[f], (FACE // 8, 128)) + RES + FACE * f
+                    )
+
+        bin_rows(pl.multiple_of(b * STEP, 8), STEP)
+        prep_step(jnp.minimum(b + 1, STEPS - 1))
+        return carry
+
+    lax.fori_loop(0, STEPS, bin_loop, 0)
 
     for c in range(4):
         for h in range(2):
@@ -691,27 +714,13 @@
             vel_out[d, pl.ds(row0, 8), :] = new[d]
             off_out[d, pl.ds(row0, 8), :] = jnp.where(live, offset, 2.0)
 
-    def look_resident(b, carry):
-        look_rows(b * KR, KR)
-        for i in range(KR // 8):
-            r = pl.multiple_of(b * KR + 8 * i, 8)
-            emit(
-                r,
-                [sol_pos[d, pl.ds(r, 8), :] for d in range(3)],
-                [sol_vel[d, pl.ds(r, 8), :] for d in range(3)],
-                sub8 + r < sol_rows[0],
-            )
-        return carry
-
-    def look_arrival(f, carry):
-        look_rows(RES + f * FACE, FACE)
-        for i in range(FACE // 8):
-            emit(
-                pl.multiple_of(RES + f * FACE + 8 * i, 8),
-                [arr_pos[d, f, 8 * i : 8 * i + 8, :] for d in range(3)],
-                [arr_vel[d, f, 8 * i : 8 * i + 8, :] for d in range(3)],
-                (sub8 + 8 * i) < arr_rows[f],
-            )
+    def emit_step(b):
+        for i in range(STEP // 8):
+            emit(*solvent(b, i))
+
+    def look_loop(b, carry):
+        emit_step(jnp.maximum(b - 1, 0))
+        look_rows(pl.multiple_of(b * STEP, 8), STEP)
         return carry
 
     look_rows(SOLV, 2)
@@ -721,38 +730,53 @@
         W_s[d] = new[d]
         speed.append(jnp.concatenate([W_s[d, 0:1, :], W_s[d, 1:2, :]], 1))
 
-    def out_copies(substep):
-        part = pl.ds(RES, SOLV - RES) if substep == 0 else pl.ds((substep - 1) * HALF, HALF)
+    def out_copies(part):
+        rows = pl.ds(part * HALF, HALF) if part < 2 else pl.ds(RES, SOLV - RES)
         return [
             pltpu.make_async_copy(
-                off_out.at[:, part], off_hbm.at[:, part], out_sem.at[0, substep]
+                off_out.at[:, rows], off_hbm.at[:, rows], out_sem.at[0, part]
             ),
             pltpu.make_async_copy(
-                vel_out.at[:, part], vel_hbm.at[:, part], out_sem.at[1, substep]
+                vel_out.at[:, rows], vel_hbm.at[:, rows], out_sem.at[1, part]
             ),
         ]
 
     half_kick = 0.5 * step_size / bead_mass
-    gone = [jnp.zeros((1, 256), F32)] * 3
-    for substep in range(3):
+
+    def substep(t, carry):
+        speed, gone, push = carry[0:3], carry[3:6], carry[6:9]
         speed = [speed[d] + half_kick * push[d] for d in range(3)]
         gone = [gone[d] + step_size * speed[d] for d in range(3)]
-        place(substep + 1, [start[d] + gone[d] for d in range(3)])
-        bead_send(substep + 1)
-        if substep == 0:
-            lax.fori_loop(0, 6, look_arrival, 0)
-        else:
-            lax.fori_loop(8 * (substep - 1), 8 * substep, look_resident, 0)
-        for copy in out_copies(substep):
-            copy.start()
-        bead_arrive(substep + 1)
-        push = forces(substep + 1)
+        place(t + 1, [start[d] + gone[d] for d in range(3)])
+        bead_send(t + 1)
+        lax.fori_loop(
+            HSTEPS * t, jnp.minimum(HSTEPS * (t + 1), STEPS), look_loop, 0
+        )
+
+        @pl.when(t == 1)
+        def _():
+            for copy in out_copies(0):
+                copy.start()
+
+        @pl.when(t == 2)
+        def _():
+            emit_step(STEPS - 1)
+            for part in (1, 2):
+                for copy in out_copies(part):
+                    copy.start()
+
+        bead_arrive(t + 1)
+        push = forces(t + 1)
         speed = [speed[d] + half_kick * push[d] for d in range(3)]
+        return (*speed, *gone, *push)
+
+    still = jnp.zeros((1, 256), F32)
+    last = lax.fori_loop(0, 3, substep, (*speed, still, still, still, *push))
     for d in range(3):
-        bpos_out[d] = gone[d]
-        bvel_out[d] = speed[d]
-    for substep in range(3):
-        for copy in out_copies(substep):
+        bpos_out[d] = last[3 + d]
+        bvel_out[d] = last[d]
+    for part in range(3):
+        for copy in out_copies(part):
             copy.wait()
 
     for g in range(6):
@@ -798,8 +822,8 @@
         in_specs=[smem] * 4 + [anywhere] * 4 + [vmem] * 5,
         out_specs=(anywhere, anywhere, vmem, vmem),
         scratch_shapes=[
-            f32(3, RES, 128),
-            f32(3, RES, 128),
+            f32(3, SOLV, 128),
+            f32(3, SOLV, 128),
             f32(3, SOLV, 128),
             f32(3, SOLV, 128),
             pltpu.VMEM((2, 1, 256), jnp.int32),
@@ -809,8 +833,7 @@
             f32(2 * TROWS, 128),
             bf(256, 128),
             bf(TROWS, 128),
-            f32(3, 6, FACE, 128),
-            f32(3, 6, FACE, 128),
+            pltpu.VMEM((72, 128), jnp.int32),
             pltpu.VMEM((6, 1, 128), jnp.int32),
             pltpu.VMEM((6, 1, 128), jnp.int32),
             f32(6, 8, 128),
@@ -854,6 +877,7 @@
             dma((4, 18)),
             dma((2, 2)),
             dma((2, 3)),
+            pltpu.SemaphoreType.REGULAR((2,)),
         ],
         compiler_params=pltpu.CompilerParams(
             collective_id=0, has_side_effects=True, vmem_limit_bytes=60 * 1024 * 1024

time: 76.5 us -> 71.3 us (0.932)
  Pallas kernels: 70.3 us -> 65.1 us
    pallas_call x1, Pallas kernels: 70.3 us -> 65.1 us  [shards(): pl.pallas_call(kernel, out_shape=(jax.ShapeDtypeStruct((3, SOLV, 128), F3...]
where the time goes in v3:
time: 71.3 us; the launch traced here: 71 us
  Pallas kernels  65.1 us (91%)
  other arithmetic  3.29 us (5%)
  between operations  1.96 us (3%)
    pallas_call x1, Pallas kernels, shards(): pl.pallas_call(kernel, out_shape=(jax.ShapeDtypeStruct((3, SOLV, 128), F3...  65.1 us
    select_n x1, other arithmetic, shards(): jnp.where(live, vel, 0.0).reshape(3, 1, 1, 1, SOLV * 128)  2.7 us

profile of v3, /device:TPU:0, one launch (start us, length us, event | category | flops | bytes accessed | tf_op | source)
XLA Modules:
  0.0 71.0 jit_solution(17638698907383024619)
XLA Ops:
  1.9 65.1 %interval.1 = (f32[3,528,128]{2,1,0:T(8,128)}, f32[3,528,128]{2,1,0:T(8,128)}, f32[3,1,256]{2,1,0:T(1,128)}, f32[3,1,256]{2,1,0:T(1,128)}) custom-call(s32[1]{0:T(128)} %bitcast.22.sol_rows, s32[6]{0:T(128)} %bitcast.34, s32[1]{0:T(128)} %bitcast.23.chains, s32[3]{0:T(128)} %shift.1, f32[3,384,128]{2,1,0:T(8,128)} %bitcast.26, f32[3,384,128]{2,1,0:T(8,128)} %bitcast.27, ...), custom_call_target="tpu_custom_call" | custom-call | tf_op jit(solution)/shard_map/interval/pallas_call | solution.py:814
  67.1 0.0 copy-start.1
  67.1 0.0 copy-start
  67.1 0.6 copy-done.1
  67.8 0.0 copy-done
  67.8 0.6 fusion.1
  68.3 2.7 %broadcast_select_fusion = (f32[3,528,128]{2,1,0:T(8,128)}, f32[3,528,128]{2,1,0:T(8,128)}) fusion(f32[3,528,128]{2,1,0:T(8,128)} %get-tuple-element.9, f32[3,528,128]{2,1,0:T(8,128)} %get-tuple-element.8), kind=kLoop, calls=%fused_computation.1 | loop fusion | flops 1013760 | bytes 3244032 | tf_op jit(solution)/shard_map/jit(_where)/select_n | solution.py:906
  (1 shorter events, 0.0 us)
Async XLA Ops:
  67.1 0.7 copy-start.1
  67.1 0.7 copy-start

commit v4 on v3

--- a/solution.py
+++ b/solution.py
@@ -44,6 +44,7 @@
     for dz in (0, 1)
     if (dx, dy, dz) != (0, 0, 0)
 ]
+OFFSETS.sort(key=lambda off: -(abs(off[0]) + abs(off[1]) + 2 * off[2]))
 FACES = [(-1, 0, 0), (1, 0, 0), (0, -1, 0), (0, 1, 0), (0, 0, 1)]
 HALO = [(1, 0, 0), (0, 1, 0), (0, 0, 1), (1, 0, 1), (0, 1, 1), (1, 1, 0), (1, 1, 1)]
 
@@ -452,7 +453,7 @@
         return copies
 
     halo = halo_copies((sx, sy, sz, se), (rx, ry, rz, re), halo_ss, halo_rs, 1)
-    for copy in halo:
+    for copy in reversed(halo):
         copy.start()
 
     row32 = lax.broadcasted_iota(jnp.int32, (32, 256), 0)
@@ -512,11 +513,11 @@
 
         def group(j, carry):
             here = []
-            for t in range(2):
-                tile = GT_s[pl.ds(pl.multiple_of(16 * j + 8 * t, 8), 8), :]
+            for t in range(8):
+                tile = GT_s[pl.ds(pl.multiple_of(64 * j + 8 * t, 8), 8), :]
                 here.append([jnp.broadcast_to(tile[:, d : d + 1], (8, 128)) for d in range(3)])
-            twice = [here[t][1] + here[t][1] for t in range(2)]
-            sums = [jnp.zeros((8, 128), F32) for i in range(6)]
+            twice = [here[t][1] + here[t][1] for t in range(8)]
+            sums = [jnp.zeros((8, 128), F32) for i in range(24)]
 
             def choose(mask, a, b):
                 return [jnp.where(mask, a[d], b[d]) for d in range(3)]
@@ -541,28 +542,28 @@
 
                 for dz in (0, 1):
                     inner = ghost_at(0, 0, dz)
-                    for t in range(2):
+                    for t in range(8):
                         add(t, inner)
                     low, high = ghost_at(0, -1, dz), ghost_at(0, 1, dz)
                     half_way = row(M_s, 4 * slot(0, -1, dz) + 1)
-                    for t in range(2):
+                    for t in range(8):
                         add(t, choose(here[t][1] < half_way, low, high))
-                    near = [[], []]
+                    near = [[] for t in range(8)]
                     for dy in (0, -1, 1):
                         low, high = ghost_at(-1, dy, dz), ghost_at(1, dy, dz)
                         half_way = row(M_s, 4 * slot(-1, dy, dz))
-                        for t in range(2):
+                        for t in range(8):
                             near[t].append(choose(here[t][0] < half_way, low, high))
-                    for t in range(2):
+                    for t in range(8):
                         side, low, high = near[t]
                         add(t, side)
                         add(t, choose(twice[t] < low[1] + high[1], low, high))
-            for t in range(2):
+            for t in range(8):
                 for d in range(3):
-                    A_s[pl.ds(pl.multiple_of(256 * d + 16 * j + 8 * t, 8), 8), :] = sums[3 * t + d]
+                    A_s[pl.ds(pl.multiple_of(256 * d + 64 * j + 8 * t, 8), 8), :] = sums[3 * t + d]
             return carry
 
-        lax.fori_loop(0, 16, group, 0)
+        lax.fori_loop(0, 4, group, 0)
         ones = jnp.ones((8, 128), BF)
         pieces = split3(A_s[...])
         pair = nt(ones, pieces[0]) + nt(ones, pieces[1]) + nt(ones, pieces[2])
@@ -642,7 +643,7 @@
             uy[2 * q + j : 2 * q + j + 1, :] = jnp.sum(vy[half], axis=0, keepdims=True)
         ue[q : q + 1, :] = jnp.sum(ve, axis=0, keepdims=True)
     info = halo_copies((ux, uy, uz, ue), (gx_, gy_, gz_, ge), info_ss, info_rs, -1)
-    for copy in info:
+    for copy in reversed(info):
         copy.start()
     for copy in halo_copies((ux, uy, uz, ue), (gx_, gy_, gz_, ge), info_ss, info_rs, 1):
         copy.wait_recv()

time: 71.3 us -> 68.3 us (0.958)
  Pallas kernels: 65.1 us -> 62.2 us
    pallas_call x1, Pallas kernels: 65.1 us -> 62.2 us  [shards(): pl.pallas_call(kernel, out_shape=(jax.ShapeDtypeStruct((3, SOLV, 128), F3...]
where the time goes in v4:
time: 68.3 us; the launch traced here: 68.1 us
  Pallas kernels  62.2 us (91%)
  other arithmetic  3.29 us (5%)
  between operations  1.96 us (3%)
    pallas_call x1, Pallas kernels, shards(): pl.pallas_call(kernel, out_shape=(jax.ShapeDtypeStruct((3, SOLV, 128), F3...  62.2 us
    select_n x1, other arithmetic, shards(): jnp.where(live, vel, 0.0).reshape(3, 1, 1, 1, SOLV * 128)  2.7 us

profile of v4, /device:TPU:0, one launch (start us, length us, event | category | flops | bytes accessed | tf_op | source)
XLA Modules:
  0.0 68.1 jit_solution(13119809993765178828)
XLA Ops:
  1.9 62.2 %interval.1 = (f32[3,528,128]{2,1,0:T(8,128)}, f32[3,528,128]{2,1,0:T(8,128)}, f32[3,1,256]{2,1,0:T(1,128)}, f32[3,1,256]{2,1,0:T(1,128)}) custom-call(s32[1]{0:T(128)} %bitcast.22.sol_rows, s32[6]{0:T(128)} %bitcast.34, s32[1]{0:T(128)} %bitcast.23.chains, s32[3]{0:T(128)} %shift.1, f32[3,384,128]{2,1,0:T(8,128)} %bitcast.26, f32[3,384,128]{2,1,0:T(8,128)} %bitcast.27, ...), custom_call_target="tpu_custom_call" | custom-call | tf_op jit(solution)/shard_map/interval/pallas_call | solution.py:815
  64.1 0.0 copy-start.1
  64.1 0.0 copy-start
  64.1 0.6 copy-done.1
  64.8 0.0 copy-done
  64.8 0.6 fusion.1
  65.4 2.7 %broadcast_select_fusion = (f32[3,528,128]{2,1,0:T(8,128)}, f32[3,528,128]{2,1,0:T(8,128)}) fusion(f32[3,528,128]{2,1,0:T(8,128)} %get-tuple-element.9, f32[3,528,128]{2,1,0:T(8,128)} %get-tuple-element.8), kind=kLoop, calls=%fused_computation.1 | loop fusion | flops 1013760 | bytes 3244032 | tf_op jit(solution)/shard_map/jit(_where)/select_n | solution.py:907
  (1 shorter events, 0.0 us)
Async XLA Ops:
  64.1 0.7 %copy-start.1 = (f32[3,1,256]{2,1,0:T(1,128)S(1)}, f32[3,1,256]{2,1,0:T(1,128)}, u32[]{:S(2)}) copy-start(f32[3,1,256]{2,1,0:T(1,128)} %get-tuple-element.11) | copy-start | bytes 9220
  64.1 0.7 copy-start

commit v5 on v4

--- a/solution.py
+++ b/solution.py
@@ -830,8 +830,8 @@
             pltpu.VMEM((2, 1, 256), jnp.int32),
             f32(ALL, 128),
             f32(ALL, 128),
-            f32(ALL * 8, 128),
-            f32(2 * TROWS, 128),
+            f32(ALL * 8 + 64, 128),
+            f32(2 * TROWS + 32, 128),
             bf(256, 128),
             bf(TROWS, 128),
             pltpu.VMEM((72, 128), jnp.int32),

time: 68.3 us -> 68.3 us (level)
  no operation moved by 1% of the time
where the time goes in v5:
time: 68.3 us; the launch traced here: 68.1 us
  Pallas kernels  62.2 us (91%)
  other arithmetic  3.29 us (5%)
  between operations  1.96 us (3%)
    pallas_call x1, Pallas kernels, shards(): pl.pallas_call(kernel, out_shape=(jax.ShapeDtypeStruct((3, SOLV, 128), F3...  62.2 us
    select_n x1, other arithmetic, shards(): jnp.where(live, vel, 0.0).reshape(3, 1, 1, 1, SOLV * 128)  2.7 us

profile of v5, /device:TPU:0, one launch (start us, length us, event | category | flops | bytes accessed | tf_op | source)
XLA Modules:
  0.0 68.1 jit_solution(17253118397792888454)
XLA Ops:
  1.9 62.2 %interval.1 = (f32[3,528,128]{2,1,0:T(8,128)}, f32[3,528,128]{2,1,0:T(8,128)}, f32[3,1,256]{2,1,0:T(1,128)}, f32[3,1,256]{2,1,0:T(1,128)}) custom-call(s32[1]{0:T(128)} %bitcast.22.sol_rows, s32[6]{0:T(128)} %bitcast.34, s32[1]{0:T(128)} %bitcast.23.chains, s32[3]{0:T(128)} %shift.1, f32[3,384,128]{2,1,0:T(8,128)} %bitcast.26, f32[3,384,128]{2,1,0:T(8,128)} %bitcast.27, ...), custom_call_target="tpu_custom_call" | custom-call | tf_op jit(solution)/shard_map/interval/pallas_call | solution.py:815
  64.1 0.0 copy-start.1
  64.1 0.0 copy-start
  64.1 0.6 copy-done.1
  64.8 0.0 copy-done
  64.8 0.6 fusion.1
  65.4 2.7 %broadcast_select_fusion = (f32[3,528,128]{2,1,0:T(8,128)}, f32[3,528,128]{2,1,0:T(8,128)}) fusion(f32[3,528,128]{2,1,0:T(8,128)} %get-tuple-element.9, f32[3,528,128]{2,1,0:T(8,128)} %get-tuple-element.8), kind=kLoop, calls=%fused_computation.1 | loop fusion | flops 1013760 | bytes 3244032 | tf_op jit(solution)/shard_map/jit(_where)/select_n | solution.py:907
  (1 shorter events, 0.0 us)
Async XLA Ops:
  64.1 0.7 %copy-start.1 = (f32[3,1,256]{2,1,0:T(1,128)S(1)}, f32[3,1,256]{2,1,0:T(1,128)}, u32[]{:S(2)}) copy-start(f32[3,1,256]{2,1,0:T(1,128)} %get-tuple-element.11) | copy-start | bytes 9220
  64.1 0.7 copy-start
